TPU v7x, 32 devices: a whole 2x2x4 slice. The times are simulated.
32 devices in a mesh: slab: 8 (over y, x, core), coil: 4 (over z).
Axes of the slice: x: 2, y: 2, z: 4, core: 2. Of those that a mesh axis runs over, the one named last changes fastest.
Arguments:
- samples: bfloat16 [8, 65536, 128], P('coil', 'slab'), may hold values from -6 to 6
- sample_pos: bfloat16 [65536, 64], P('slab'), may hold values from 0 to 64
- block_count: int32 [65536], P('slab'), may hold values from 16 to 64
- grid_block: int32 [65536], P('slab'), may hold values from 0 to 32767
- block_slab: int32 [65536, 1], P('slab'), may hold values from 0 to 7, as said below
- sensitivity: bfloat16 [8, 256, 16, 512], P(None, 'slab', 'coil'), may hold values from -3 to 3
Outputs:
- image: float32 [256, 16, 512], P('slab', 'coil')
Inputs may be any that keep to these rules, and one draw needn't show every extreme that they name: `block_slab`: within the rows of one device no slab is named more than 2560 times; one slab, the same for every device, is named exactly 2560 times by every device.
All inputs are finite; a program needn't handle non-finite values.
Results may differ from a plain program's by a relative error of at most 0.02.
The roundings to bfloat16 on the way count: a program that leaves them out, or rounds other values in their place, can miss the bound.
Values may be sent and summed in bfloat16 or wider, within the bound.
A program may use at most 128 MiB of HBM per device.

v0:
```python
import math

import jax
import jax.numpy as jnp
from jax import lax
from jax.sharding import PartitionSpec as P

KX = 256


kernel_half = 2.5


def block_weights(positions, counts):
    cell_mid = jnp.arange(positions.shape[-1], dtype=jnp.int32).astype(jnp.float32) + 0.5
    offset = (positions.astype(jnp.float32)[..., :, None] - cell_mid) / kernel_half
    bump = jnp.maximum(1.0 - offset * offset, 0.0)
    live = jnp.arange(positions.shape[-1], dtype=jnp.int32)[:, None] < counts[..., None, None]
    return jnp.where(live, bump * bump, 0.0).astype(jnp.bfloat16)


def twiddle(first, second, length):
    phase = (first * second % length).astype(jnp.float32) * (2.0 * math.pi / length)
    scale = 1.0 / math.sqrt(length)
    return (jnp.cos(phase) * scale, jnp.sin(phase) * scale)


def choose(part_in, part_out, cosine, sine):
    upper = jnp.where(part_out == 0, cosine, sine)
    lower = jnp.where(part_out == 0, -sine, cosine)
    return jnp.where(part_in == 0, upper, lower).astype(jnp.bfloat16)


def across_table(kx_len, rows_out):
    index_in = jnp.arange(2 * kx_len, dtype=jnp.int32)
    segment = index_in // 128
    part_in = index_in // 64 % 2
    cell_at = segment * 64 + index_in % 64
    index_out = jnp.arange(2 * rows_out, dtype=jnp.int32)
    part_out = index_out // rows_out
    row_at = (kx_len - rows_out) // 2 + index_out % rows_out
    cosine, sine = twiddle(cell_at[:, None], row_at[None, :], kx_len)
    return choose(part_in[:, None], part_out[None, :], cosine, sine)


def square_table(length):
    index_in = jnp.arange(2 * length, dtype=jnp.int32)
    index_out = jnp.arange(2 * length, dtype=jnp.int32)
    cosine, sine = twiddle((index_in // 2)[:, None], (index_out % length)[None, :], length)
    return choose((index_in % 2)[:, None], (index_out // length)[None, :], cosine, sine)


def depth_table(positions, freqs, length):
    cosine, sine = twiddle(positions[:, None], freqs[None, :], length)
    upper = jnp.stack([cosine, -sine], axis=-1)
    lower = jnp.stack([sine, cosine], axis=-1)
    return jnp.stack([upper, lower], axis=1).astype(jnp.bfloat16)


def conj_sum(coil_maps, coil_images, half):
    map_re = coil_maps[..., :half].astype(jnp.float32)
    map_im = coil_maps[..., half:].astype(jnp.float32)
    img_re = coil_images[..., :half].astype(jnp.float32)
    img_im = coil_images[..., half:].astype(jnp.float32)
    real_part = jnp.sum(map_re * img_re + map_im * img_im, axis=1)
    imag_part = jnp.sum(map_re * img_im - map_im * img_re, axis=1)
    return jnp.concatenate([real_part, imag_part], axis=-1)


def grid_samples(values, positions, counts):
    row_total = values.shape[0]
    group_len = math.gcd(row_total, 1024)
    coil_count = values.shape[1] // 128

    def one_group(pieces):
        group_vals, group_pos, group_cnt = pieces
        weights = block_weights(group_pos, group_cnt)
        shaped = group_vals.reshape(group_len, coil_count, 2, 64)
        result = jnp.einsum("mij,mcpi->mcpj", weights, shaped, preferred_element_type=jnp.float32)
        return result.reshape(group_len, coil_count * 128).astype(jnp.bfloat16)

    grouped = (
        values.reshape(row_total // group_len, group_len, values.shape[1]),
        positions.reshape(row_total // group_len, group_len, positions.shape[1]),
        counts.reshape(row_total // group_len, group_len),
    )
    return lax.map(one_group, grouped).reshape(row_total, values.shape[1])


def pack_rows(block_slab, slab_total, capacity, members):
    dest_slab = block_slab[:, 0]
    onehot = (dest_slab[:, None] == jnp.arange(slab_total, dtype=jnp.int32)[None, :]).astype(
        jnp.int32
    )
    before = jnp.cumsum(onehot, axis=0) - onehot
    rank_row = jnp.sum(before * onehot, axis=1)
    slot_index = dest_slab * capacity + rank_row
    packed = []
    for member in members:
        buffer = (
            jnp.zeros((slab_total * capacity,) + member.shape[1:], member.dtype)
            .at[slot_index]
            .set(member)
        )
        packed.append(buffer.reshape((slab_total, capacity) + member.shape[1:]))
    return tuple(packed)


def per_device(samples, sample_pos, block_count, grid_block, block_slab, sensitivity):
    slab_total = lax.axis_size("slab")
    coils_here = samples.shape[0]
    blocks_here = samples.shape[1]
    capacity = 5 * blocks_here // (2 * slab_total)
    planes = sensitivity.shape[1]
    width_rows = sensitivity.shape[2] * lax.axis_size("coil")
    depth_len = planes * slab_total
    freq_len = sensitivity.shape[3] // 2
    seg_count = KX // 64
    values = jnp.transpose(samples, (1, 0, 2)).reshape(blocks_here, coils_here * 128)
    local_cells = grid_samples(values, sample_pos, block_count)
    sent_cells, sent_segment = pack_rows(
        block_slab, slab_total, capacity, (local_cells, grid_block[:, None])
    )
    cell_rows, segment_wide = (
        lax.all_to_all(sent_cells, "slab", split_axis=0, concat_axis=0, tiled=True),
        lax.all_to_all(sent_segment, "slab", split_axis=0, concat_axis=0, tiled=True),
    )
    segment_of = segment_wide[:, :, 0]
    grid_rows = planes * freq_len * seg_count
    cell_wide = lax.optimization_barrier(cell_rows).astype(jnp.float32)
    kspace = (
        jnp.zeros((grid_rows, cell_rows.shape[2]), jnp.float32)
        .at[segment_of.reshape(-1)]
        .add(cell_wide.reshape(-1, cell_rows.shape[2]))
    )
    kspace = kspace.astype(jnp.bfloat16).reshape(planes * freq_len, seg_count, coils_here, 128)
    across = across_table(KX, width_rows).reshape(seg_count, 128, 2 * width_rows)
    x_rows = jnp.einsum("rscf,sfn->rcn", kspace, across, preferred_element_type=jnp.float32).astype(
        jnp.bfloat16
    )
    x_rows = x_rows.reshape(planes, freq_len, coils_here, 2, width_rows)
    y_table = square_table(freq_len).reshape(freq_len, 2, 2 * freq_len)
    y_planes = jnp.einsum(
        "zkcqx,kqn->zcxn", x_rows, y_table, preferred_element_type=jnp.float32
    ).astype(jnp.bfloat16)
    shaped = y_planes.reshape(planes, coils_here, width_rows, 2, freq_len)
    own_planes = lax.axis_index("slab") * planes + jnp.arange(planes, dtype=jnp.int32)
    table = depth_table(
        jnp.arange(lax.axis_size("slab") * planes, dtype=jnp.int32), own_planes, depth_len
    )
    result = jnp.einsum("zpkq,kcxqy->zcxpy", table, shaped, preferred_element_type=jnp.float32)
    coil_image = lax.psum_scatter(
        result.reshape(lax.axis_size("slab") * planes, coils_here, width_rows, 2 * freq_len).astype(
            jnp.bfloat16
        ),
        "slab",
        scatter_dimension=0,
        tiled=True,
    )
    coil_index = lax.axis_index("coil")
    own_maps = lax.dynamic_slice_in_dim(
        lax.all_gather(sensitivity, "coil", axis=2, tiled=True),
        coil_index * coils_here,
        coils_here,
        0,
    )
    partial_sum = conj_sum(jnp.swapaxes(own_maps, 0, 1), coil_image, freq_len)
    image = lax.psum_scatter(
        partial_sum.astype(jnp.bfloat16), "coil", scatter_dimension=1, tiled=True
    ).astype(jnp.float32)
    return image


def solution(mesh):
    return jax.shard_map(
        per_device,
        mesh=mesh,
        in_specs=(
            P("coil", "slab", None),
            P("slab", None),
            P("slab"),
            P("slab"),
            P("slab", None),
            P(None, "slab", "coil", None),
        ),
        out_specs=P("slab", "coil", None),
        check_vma=False,
    )
```

profile of v0, /device:TPU:0, one launch (start us, length us, event | category | flops | bytes accessed | tf_op | source)
XLA Modules:
  0.0 837.4 jit_solution(13076570309176219995)
XLA Ops:
  8.1 2.4 reduce-window.6
  11.2 1.0 fusion.45
  13.0 31.3 %scatter_custom_fusion = s32[20480]{0:T(1024)} fusion(s32[8192]{0:T(1024)S(1)} %bitcast.135, s32[8192]{0:T(1024)} %param.11, s32[]{:T(128)} %constant.200.clone.1), kind=kCustom, calls=%fused_computation.85 | custom fusion | bytes 82432 | tf_op jit(solution)/shard_map/scatter | solution.py:103
  44.3 5.2 all-to-all-start
  49.5 6.4 copy.33
  55.9 6.6 copy.63
  62.5 4.3 copy.35
  66.7 1.8 copy.34
  68.6 278.2 %while.10 = (s32[]{:T(128)}, bf16[8,1024,256]{2,1,0:T(8,128)(2,1)}, bf16[8,1024,256]{1,2,0:T(8,128)(2,1)}, s32[8,1024]{1,0:T(8,128)S(1)}, bf16[8,1024,64]{2,1,0:T(8,128)(2,1)}, /*index=5*/s32[]{:T(128)}) while((s32[]{:T(128)}, bf16[8,1024,256]{2,1,0:T(8,128)(2,1)}, bf16[8,1024,256]{1,2,0:T(8,128)(2,1)}, s32[8,1024]{1,0:T(8,128)S(1)}, ...), condition=%wide.region_5.6_spmd, body=%wide.region_4.5_spmd.sunk | while | flops 67502208 | bytes 7091281 | solution.py:87
  68.6 1.1 constant_dynamic-slice_fusion.4
  70.5 1.0 bitcast_convert_fusion.4
  71.7 29.2 %fusion.112 = bf16[1024,2,2,64]{3,2,1,0:T(2,128)(2,1)S(1)} fusion(bf16[1024,2,2,64]{3,2,1,0:T(2,128)(2,1)S(1)} %copy.84, f32[64]{0:T(128)S(1)} %convert_add_fusion.2, f32[1024,64]{1,0:T(8,128)S(1)} %bitcast_convert_fusion.4, pred[1024,64]{1,0:T(8,128)(4,1)S(1)} %iota_compare_fusion.4), kind=kOutput, calls=%fused_computation.7.clone.2 | convolution fusion | flops 67371008 | bytes 1376512 | tf_op jit(solution)/shard_map/while/body/eval_jaxpr/mij,mcpi->mcpj/dot_general | solution.py:79
  100.9 1.4 copy.85
  102.5 0.9 constant_dynamic-update-slice_fusion.2
  103.4 1.1 constant_dynamic-slice_fusion.4
  105.2 1.0 bitcast_convert_fusion.4
  106.5 29.2 %fusion.112 = bf16[1024,2,2,64]{3,2,1,0:T(2,128)(2,1)S(1)} fusion(bf16[1024,2,2,64]{3,2,1,0:T(2,128)(2,1)S(1)} %copy.84, f32[64]{0:T(128)S(1)} %convert_add_fusion.2, f32[1024,64]{1,0:T(8,128)S(1)} %bitcast_convert_fusion.4, pred[1024,64]{1,0:T(8,128)(4,1)S(1)} %iota_compare_fusion.4), kind=kOutput, calls=%fused_computation.7.clone.2 | convolution fusion | flops 67371008 | bytes 1376512 | tf_op jit(solution)/shard_map/while/body/eval_jaxpr/mij,mcpi->mcpj/dot_general | solution.py:79
  135.7 1.4 copy.85
  137.3 0.8 constant_dynamic-update-slice_fusion.2
  138.1 1.1 constant_dynamic-slice_fusion.4
  140.0 1.0 bitcast_convert_fusion.4
  141.2 29.2 %fusion.112 = bf16[1024,2,2,64]{3,2,1,0:T(2,128)(2,1)S(1)} fusion(bf16[1024,2,2,64]{3,2,1,0:T(2,128)(2,1)S(1)} %copy.84, f32[64]{0:T(128)S(1)} %convert_add_fusion.2, f32[1024,64]{1,0:T(8,128)S(1)} %bitcast_convert_fusion.4, pred[1024,64]{1,0:T(8,128)(4,1)S(1)} %iota_compare_fusion.4), kind=kOutput, calls=%fused_computation.7.clone.2 | convolution fusion | flops 67371008 | bytes 1376512 | tf_op jit(solution)/shard_map/while/body/eval_jaxpr/mij,mcpi->mcpj/dot_general | solution.py:79
  170.4 1.4 copy.85
  172.0 0.8 constant_dynamic-update-slice_fusion.2
  172.9 1.1 constant_dynamic-slice_fusion.4
  174.7 1.0 bitcast_convert_fusion.4
  176.0 29.2 %fusion.112 = bf16[1024,2,2,64]{3,2,1,0:T(2,128)(2,1)S(1)} fusion(bf16[1024,2,2,64]{3,2,1,0:T(2,128)(2,1)S(1)} %copy.84, f32[64]{0:T(128)S(1)} %convert_add_fusion.2, f32[1024,64]{1,0:T(8,128)S(1)} %bitcast_convert_fusion.4, pred[1024,64]{1,0:T(8,128)(4,1)S(1)} %iota_compare_fusion.4), kind=kOutput, calls=%fused_computation.7.clone.2 | convolution fusion | flops 67371008 | bytes 1376512 | tf_op jit(solution)/shard_map/while/body/eval_jaxpr/mij,mcpi->mcpj/dot_general | solution.py:79
  205.2 1.4 copy.85
  206.8 0.8 constant_dynamic-update-slice_fusion.2
  207.6 1.1 constant_dynamic-slice_fusion.4
  209.5 1.0 bitcast_convert_fusion.4
  210.7 29.2 %fusion.112 = bf16[1024,2,2,64]{3,2,1,0:T(2,128)(2,1)S(1)} fusion(bf16[1024,2,2,64]{3,2,1,0:T(2,128)(2,1)S(1)} %copy.84, f32[64]{0:T(128)S(1)} %convert_add_fusion.2, f32[1024,64]{1,0:T(8,128)S(1)} %bitcast_convert_fusion.4, pred[1024,64]{1,0:T(8,128)(4,1)S(1)} %iota_compare_fusion.4), kind=kOutput, calls=%fused_computation.7.clone.2 | convolution fusion | flops 67371008 | bytes 1376512 | tf_op jit(solution)/shard_map/while/body/eval_jaxpr/mij,mcpi->mcpj/dot_general | solution.py:79
  239.9 1.4 copy.85
  241.6 0.9 constant_dynamic-update-slice_fusion.2
  242.4 1.1 constant_dynamic-slice_fusion.4
  244.3 1.0 bitcast_convert_fusion.4
  245.5 29.2 %fusion.112 = bf16[1024,2,2,64]{3,2,1,0:T(2,128)(2,1)S(1)} fusion(bf16[1024,2,2,64]{3,2,1,0:T(2,128)(2,1)S(1)} %copy.84, f32[64]{0:T(128)S(1)} %convert_add_fusion.2, f32[1024,64]{1,0:T(8,128)S(1)} %bitcast_convert_fusion.4, pred[1024,64]{1,0:T(8,128)(4,1)S(1)} %iota_compare_fusion.4), kind=kOutput, calls=%fused_computation.7.clone.2 | convolution fusion | flops 67371008 | bytes 1376512 | tf_op jit(solution)/shard_map/while/body/eval_jaxpr/mij,mcpi->mcpj/dot_general | solution.py:79
  274.7 1.4 copy.85
  276.3 0.9 constant_dynamic-update-slice_fusion.2
  277.2 1.1 constant_dynamic-slice_fusion.4
  279.1 1.0 bitcast_convert_fusion.4
  280.3 29.2 %fusion.112 = bf16[1024,2,2,64]{3,2,1,0:T(2,128)(2,1)S(1)} fusion(bf16[1024,2,2,64]{3,2,1,0:T(2,128)(2,1)S(1)} %copy.84, f32[64]{0:T(128)S(1)} %convert_add_fusion.2, f32[1024,64]{1,0:T(8,128)S(1)} %bitcast_convert_fusion.4, pred[1024,64]{1,0:T(8,128)(4,1)S(1)} %iota_compare_fusion.4), kind=kOutput, calls=%fused_computation.7.clone.2 | convolution fusion | flops 67371008 | bytes 1376512 | tf_op jit(solution)/shard_map/while/body/eval_jaxpr/mij,mcpi->mcpj/dot_general | solution.py:79
  309.5 1.4 copy.85
  312.0 1.1 constant_dynamic-slice_fusion.4
  313.8 1.0 bitcast_convert_fusion.4
  315.1 29.2 %fusion.112 = bf16[1024,2,2,64]{3,2,1,0:T(2,128)(2,1)S(1)} fusion(bf16[1024,2,2,64]{3,2,1,0:T(2,128)(2,1)S(1)} %copy.84, f32[64]{0:T(128)S(1)} %convert_add_fusion.2, f32[1024,64]{1,0:T(8,128)S(1)} %bitcast_convert_fusion.4, pred[1024,64]{1,0:T(8,128)(4,1)S(1)} %iota_compare_fusion.4), kind=kOutput, calls=%fused_computation.7.clone.2 | convolution fusion | flops 67371008 | bytes 1376512 | tf_op jit(solution)/shard_map/while/body/eval_jaxpr/mij,mcpi->mcpj/dot_general | solution.py:79
  344.3 1.4 copy.85
  345.9 0.8 constant_dynamic-update-slice_fusion.2
  346.7 41.7 %scatter_custom_fusion.1 = bf16[20480,256]{1,0:T(8,128)(2,1)} fusion(s32[8192]{0:T(1024)S(1)} %bitcast.136, bf16[8192,256]{1,0:T(8,128)(2,1)} %bitcast.138, bf16[]{:T(256)} %constant.206.clone.1), kind=kCustom, calls=%fused_computation.25 | custom fusion | bytes 10486272 | tf_op jit(solution)/shard_map/scatter | solution.py:103
  388.4 5.3 all-to-all-start.1
  393.8 1.2 copy.31
  395.5 114.7 %all-to-all-done.1 = bf16[8,2560,256]{2,1,0:T(8,128)(2,1)} async-done(((bf16[8,2560,256]{2,1,0:T(8,128)(2,1)}), bf16[8,2560,256]{2,1,0:T(8,128)(2,1)}, u32[]{:S(2)}, u32[]{:S(2)}) %all-to-all-start.1) | async-done | bytes 10485792 | tf_op jit(solution)/shard_map/all_to_all | solution.py:125
  510.2 113.7 %scatter_custom_fusion.2 = f32[32768,256]{1,0:T(8,128)} fusion(s32[20480]{0:T(1024)S(1)} %bitcast.134, bf16[20480,256]{1,0:T(8,128)(2,1)} %bitcast.41, f32[]{:T(128)} %constant.202.clone.1), kind=kCustom, calls=%fused_computation.17 | custom fusion | flops 10485760 | bytes 44040196 | tf_op jit(solution)/shard_map/scatter-add | solution.py:134
  624.0 17.1 %convert_element_type.121 = bf16[32768,256]{1,0:T(8,128)(2,1)} convert(f32[32768,256]{1,0:T(8,128)} %scatter_custom_fusion.2) | non-fusion elementwise | flops 8388608 | bytes 50331648 | tf_op jit(solution)/shard_map/convert_element_type | solution.py:136
  641.1 23.7 %reshape.478 = bf16[8192,4,2,128]{3,2,1,0:T(2,128)(2,1)} reshape(bf16[32768,256]{1,0:T(8,128)(2,1)} %convert_element_type.121) | data formatting | bytes 33554432 | tf_op jit(solution)/shard_map/reshape | solution.py:136
  664.8 11.9 %fusion.18 = bf16[8192,2,32]{0,2,1:T(8,128)(2,1)S(1)} fusion(bf16[8192,4,2,128]{3,2,1,0:T(2,128)(2,1)} %reshape.478, s32[32]{0:T(128)S(1)} %fusion.89, s32[4,128]{1,0:T(4,128)S(1)} %fusion.77, pred[32]{0:T(512)(128)(4,1)S(1)} %fusion.90, pred[4,128]{1,0:T(4,128)(4,1)S(1)} %fusion.75), kind=kOutput, calls=%fused_computation.24 | convolution fusion | flops 537739264 | bytes 17828512 | tf_op jit(solution)/shard_map/rscf,sfn->rcn/dot_general | solution.py:138
  677.0 5.2 bitcast_convert_fusion.2
  682.7 5.6 bitcast_convert_fusion.1
  688.3 11.9 %copy.56 = bf16[256,16384]{1,0:T(8,128)(2,1)} copy(bf16[256,16384]{0,1:T(8,128)(2,1)} %bitcast.119) | data formatting | bytes 16777216
  700.2 1.3 dynamic-slice_bitcast_fusion
  701.6 101.1 %reduce-scatter.8.cloned.1.call-done = bf16[32,16384]{1,0:T(8,128)(2,1)} async-done(((bf16[256,16384]{1,0:T(8,128)(2,1)}), bf16[32,16384]{1,0:T(8,128)(2,1)}) %reduce-scatter.8.cloned.1.call-update) | async-done | bytes 1048592
  802.6 1.5 copy.65
  806.0 22.0 %reduce-scatter.6.cloned.1.call-done = bf16[32,4,512]{2,0,1:T(8,128)(2,1)} async-done(((bf16[32,16,512]{2,0,1:T(8,128)(2,1)}), bf16[32,4,512]{2,0,1:T(8,128)(2,1)}) %reduce-scatter.6.cloned.1.call-update) | async-done | bytes 131088 | tf_op jit(solution)/shard_map/reduce_scatter | solution.py:168
  828.0 1.7 copy.43
  (79 shorter events, 15.9 us)
Async XLA Ops:
  44.3 344.1 %all-to-all-start = ((s32[8,2560,1]{1,2,0:T(1,128)}), s32[8,2560,1]{1,2,0:T(1,128)S(1)}, u32[]{:S(2)}, u32[]{:S(2)}) async-start(s32[8,2560,1]{1,2,0:T(1,128)} %bitcast.12), calls=%async_computation | async-start | bytes 163840 | tf_op jit(solution)/shard_map/all_to_all | solution.py:126
  55.9 10.9 %copy-start = (bf16[8192,64]{0,1:T(8,128)(2,1)S(1)}, bf16[8192,64]{0,1:T(8,128)(2,1)}, u32[]{:S(2)}) copy-start(bf16[8192,64]{0,1:T(8,128)(2,1)} %param.9) | copy-start | bytes 3145732
  55.9 12.7 %copy-start.2 = (s32[8192]{0:T(1024)S(1)}, s32[8192]{0:T(1024)}, u32[]{:S(2)}) copy-start(s32[8192]{0:T(1024)} %param.10) | copy-start | bytes 98308
  388.4 5.3 copy-start.1
  388.4 121.8 %all-to-all-start.1 = ((bf16[8,2560,256]{2,1,0:T(8,128)(2,1)}), bf16[8,2560,256]{2,1,0:T(8,128)(2,1)}, u32[]{:S(2)}, u32[]{:S(2)}) async-start(bf16[8,2560,256]{2,1,0:T(8,128)(2,1)} %bitcast.118), calls=%async_computation.1 | async-start | bytes 20971520 | tf_op jit(solution)/shard_map/all_to_all | solution.py:125
  393.7 306.5 %all-gather.2.cloned.1.call-start = ((), (), s32[]{:S(2)}) async-start(), calls=%async_computation.4 | async-start | bytes 5242880 | tf_op jit(solution)/shard_map/all_gather | solution.py:162
  395.0 407.7 %reduce-scatter.8.cloned.1.call-start = ((), (), s32[]{:S(2)}) async-start(), calls=%async_computation.6 | async-start | bytes 9437184
  700.2 127.9 %reduce-scatter.6.cloned.1.call-start = ((), (), s32[]{:S(2)}) async-start(), calls=%async_computation.5 | async-start | bytes 655360 | tf_op jit(solution)/shard_map/reduce_scatter | solution.py:168
Sparse Core Ops, SparseCore 0:
  396.1 82.4 all-gather.1
  806.1 21.8 reduce-scatter.5
Sparse Core Ops, SparseCore 1:
  700.2 102.3 reduce-scatter.7
where the time goes:
time: 848 us; the launch traced here: 837 us
  matrix products  256 us (30%)
  waiting for transfers between devices  238 us (28%)
  local copies, waits for them, and re-layouts  169 us (20%)
  other arithmetic  148 us (17%)
  between operations  15.3 us (2%)
  starting transfers between devices  10.6 us (1%)
    dot_general x8, matrix products, one_group(): jnp.einsum('mij,mcpi->mcpj', weights, shaped, preferred_element_type=jnp....  233 us
    all_to_all x1, waiting for transfers between devices, per_device(): lax.all_to_all(sent_cells, 'slab', split_axis=0, concat_axis=0, tiled=True)  115 us
    scatter-add x1, other arithmetic, per_device(): kspace = jnp.zeros((grid_rows, cell_rows.shape[2]), jnp.float32).at[segme...  114 us
    unnamed x4, waiting for transfers between devices  101 us
    scatter x2, local copies, waits for them, and re-layouts, pack_rows(): buffer = jnp.zeros((slab_total * capacity,) + member.shape[1:], member.dt...  73 us
    reshape x1, local copies, waits for them, and re-layouts, per_device(): kspace.astype(jnp.bfloat16)  23.7 us
    unnamed x12, local copies, waits for them, and re-layouts  23.3 us
    reduce_scatter x1, waiting for transfers between devices, per_device(): lax.psum_scatter(partial_sum.astype(jnp.bfloat16), 'coil', scatter_dimens...  22 us
  transfers between devices with their start and end apart: 5, of which 3 were waited for; matrix products, arithmetic and copies ran while one was open for 63% of the time, Pallas kernels for 0%

commit v1 on v0

v1 whole, which is shorter than its diff:
```python
import functools
import math

import jax
import jax.numpy as jnp
from jax import lax
from jax.experimental import pallas as pl
from jax.experimental.pallas import tpu as pltpu
from jax.sharding import PartitionSpec as P

KX = 256
CELLS = 64
NT = (((1,), (1,)), ((), ()))


def twiddle(first, second, length):
    phase = (first * second % length).astype(jnp.float32) * (2.0 * math.pi / length)
    scale = 1.0 / math.sqrt(length)
    return (jnp.cos(phase) * scale, jnp.sin(phase) * scale)


def ints(count):
    return jnp.arange(count, dtype=jnp.int32)


def across_stack(rows_out, stacked):
    x0 = (KX - rows_out) // 2
    cosine, sine = twiddle(x0 + ints(rows_out)[:, None], ints(CELLS)[None, :], KX)
    table = jnp.concatenate([cosine, sine], axis=0)
    eye = jnp.eye(stacked, dtype=jnp.float32)
    full = eye[:, None, :, None] * table[None, :, None, :]
    return full.reshape(stacked * 2 * rows_out, stacked * CELLS).astype(jnp.bfloat16)


def right_table(length):
    cosine, sine = twiddle(ints(length)[:, None], ints(length)[None, :], length)
    upper = jnp.concatenate([cosine, sine], axis=1)
    lower = jnp.concatenate([-sine, cosine], axis=1)
    return jnp.concatenate([upper, lower], axis=0).astype(jnp.bfloat16)


def left_table(length):
    cosine, sine = twiddle(ints(length)[:, None], ints(length)[None, :], length)
    upper = jnp.concatenate([cosine, -sine], axis=1)
    lower = jnp.concatenate([sine, cosine], axis=1)
    return jnp.concatenate([upper, lower], axis=0).astype(jnp.bfloat16)


def grid_kernel(stacked, coils, rows_out, pos_ref, val_ref, seg_ref, tab_ref, out_ref, wide):
    lanes = pos_ref.shape[1]
    wide[...] = val_ref[...].astype(jnp.float32)
    mid = (lax.broadcasted_iota(jnp.int32, (CELLS, lanes), 0).astype(jnp.float32) + 0.5) * 0.4
    table = tab_ref[...]

    def step(at, sums):
        parts = []
        for k in range(stacked):
            offset = pos_ref[pl.ds(at * stacked + k, 1), :] - mid
            bump = jnp.maximum(1.0 - offset * offset, 0.0)
            parts.append((bump * bump).astype(jnp.bfloat16))
        moved = jnp.dot(
            table, jnp.concatenate(parts, axis=0), preferred_element_type=jnp.float32
        )
        sums = list(sums)
        for k in range(stacked):
            base = k * 2 * rows_out
            cosine = moved[base : base + rows_out]
            sine = moved[base + rows_out : base + 2 * rows_out]
            for c in range(coils):
                re = wide[c, pl.ds(at * stacked + k, 1), :]
                im = wide[c, pl.ds(CELLS + at * stacked + k, 1), :]
                sums[2 * c] = sums[2 * c] + (re * cosine - im * sine)
                sums[2 * c + 1] = sums[2 * c + 1] + (re * sine + im * cosine)
        return tuple(sums)

    zero = jnp.zeros((rows_out, lanes), jnp.float32)
    sums = lax.fori_loop(0, CELLS // stacked, step, (zero,) * (2 * coils))
    x_at = lax.broadcasted_iota(jnp.int32, (rows_out, lanes), 0) + (KX - rows_out) // 2
    turn = (x_at * seg_ref[...]) & 3
    for c in range(coils):
        re, im = sums[2 * c], sums[2 * c + 1]
        new_re = jnp.where((turn & 1) == 0, re, -im)
        new_im = jnp.where((turn & 1) == 0, im, re)
        sign = jnp.where(turn >= 2, -1.0, 1.0)
        out_ref[2 * c] = (new_re * sign).astype(jnp.bfloat16)
        out_ref[2 * c + 1] = (new_im * sign).astype(jnp.bfloat16)


def sort_kernel(vals_ref, rank_ref, out_ref):
    group = vals_ref.shape[1]
    tile = min(256, group)

    @pl.loop(0, group // tile)
    def _(at):
        start = pl.multiple_of(at * tile, tile)
        slot = lax.broadcasted_iota(jnp.int32, (tile, group), 0) + start
        hot = jnp.where(slot == rank_ref[...], 1.0, 0.0).astype(jnp.bfloat16)
        moved = lax.dot_general(vals_ref[...], hot, NT, preferred_element_type=jnp.float32)
        out_ref[:, pl.ds(start, tile)] = moved.astype(jnp.bfloat16)


def add_kernel(
    chunk, span, lo_ref, hi_ref, vals_ref, kz_ref, ky_ref, ytab_ref, ztab_ref, out_ref, total
):
    step = pl.program_id(0)
    rows = vals_ref.shape[1]
    width = vals_ref.shape[2]
    depth, freq = total.shape[1], total.shape[2]

    @pl.when(step == 0)
    def _():
        total[...] = jnp.zeros_like(total)

    for part in range(width // chunk):
        cut = slice(part * chunk, (part + 1) * chunk)
        spot = lax.broadcasted_iota(jnp.int32, (freq, chunk), 0)
        hot = jnp.where(spot == ky_ref[0, :, cut], 1.0, 0.0).astype(jnp.bfloat16)
        plane = lax.broadcasted_iota(jnp.int32, (span, chunk), 0)
        kz = kz_ref[0, :, cut]
        vals = [vals_ref[0, v : v + 1, cut].astype(jnp.float32) for v in range(rows)]
        at_chunk = step * (width // chunk) + part

        def one(at, carry):
            start = pl.multiple_of(at * span, span)
            mine = plane == (kz - start)
            left = jnp.concatenate(
                [jnp.where(mine, vals[v], 0.0).astype(jnp.bfloat16) for v in range(rows)], axis=0
            )
            moved = lax.dot_general(left, hot, NT, preferred_element_type=jnp.float32)
            for v in range(rows):
                total[v, pl.ds(start, span), :] += moved[v * span : (v + 1) * span]
            return carry

        lax.fori_loop(lo_ref[at_chunk], hi_ref[at_chunk], one, 0)

    @pl.when(step == pl.num_programs(0) - 1)
    def _():
        pairs = rows // 2
        for pair in range(pairs):
            both = jnp.concatenate([total[2 * pair], total[2 * pair + 1]], axis=1)
            planes = jnp.dot(
                both.astype(jnp.bfloat16), ytab_ref[...], preferred_element_type=jnp.float32
            ).astype(jnp.bfloat16)
            planes = jnp.concatenate([planes[:, :freq], planes[:, freq:]], axis=0)
            image = jnp.dot(ztab_ref[...], planes, preferred_element_type=jnp.float32)
            out_ref[pair, :, :freq] = image[:depth].astype(jnp.bfloat16)
            out_ref[pair, :, freq:] = image[depth:].astype(jnp.bfloat16)


def whole(memory=pltpu.VMEM):
    return pl.BlockSpec(memory_space=memory)


def per_device(samples, sample_pos, block_count, grid_block, block_slab, sensitivity):
    slab_total = lax.axis_size("slab")
    coil_total = lax.axis_size("coil")
    coils = samples.shape[0]
    blocks = samples.shape[1]
    planes = sensitivity.shape[1]
    rows_out = sensitivity.shape[2] * coil_total
    depth = planes * slab_total
    freq = sensitivity.shape[3] // 2
    x_here = rows_out // slab_total
    segments = KX // CELLS

    live = ints(CELLS)[:, None] < block_count[None, :]
    pos = jnp.where(live, sample_pos.T.astype(jnp.float32), 1.0e4) * 0.4
    vals = jnp.swapaxes(samples, 1, 2)
    seg = (grid_block % segments)[None, :]
    kz = block_slab[:, 0] * planes + grid_block // (segments * freq)
    ky = grid_block // segments % freq

    stacked = 4
    tile = math.gcd(blocks, 256)
    table = across_stack(rows_out, stacked)
    spread = pl.pallas_call(
        functools.partial(grid_kernel, stacked, coils, rows_out),
        grid=(blocks // tile,),
        in_specs=[
            pl.BlockSpec((CELLS, tile), lambda b: (0, b)),
            pl.BlockSpec((coils, 2 * CELLS, tile), lambda b: (0, 0, b)),
            pl.BlockSpec((1, tile), lambda b: (0, b)),
            pl.BlockSpec(table.shape, lambda b: (0, 0)),
        ],
        out_specs=pl.BlockSpec((2 * coils, rows_out, tile), lambda b: (0, 0, b)),
        out_shape=jax.ShapeDtypeStruct((2 * coils, rows_out, blocks), jnp.bfloat16),
        scratch_shapes=[pltpu.VMEM((coils, 2 * CELLS, tile), jnp.float32)],
        name="grid_x",
    )(pos, vals, seg, table)

    group = math.gcd(blocks, 2048)
    groups = blocks // group
    key = (kz * group + ints(blocks) % group).reshape(groups, group)
    rank = jnp.sum((key[:, :, None] < key[:, None, :]).astype(jnp.int32), axis=1)
    rank = rank.reshape(1, blocks)
    lines = spread.reshape(coils, 2, slab_total, x_here, blocks)
    lines = jnp.transpose(lines, (2, 0, 3, 1, 4)).reshape(2 * coils * rows_out, blocks)
    spots = jnp.stack([kz, ky]).astype(jnp.bfloat16)
    lines = jnp.concatenate([lines, jnp.pad(spots, ((0, 14), (0, 0)))], axis=0)
    ordered = pl.pallas_call(
        sort_kernel,
        grid=(groups,),
        in_specs=[
            pl.BlockSpec((lines.shape[0], group), lambda b: (0, b)),
            pl.BlockSpec((1, group), lambda b: (0, b)),
        ],
        out_specs=pl.BlockSpec((lines.shape[0], group), lambda b: (0, b)),
        out_shape=jax.ShapeDtypeStruct(lines.shape, jnp.bfloat16),
        name="order_kz",
    )(lines, rank)
    count = 2 * coils * rows_out
    each = 2 * coils * x_here
    sent = lax.all_to_all(
        ordered[:count].reshape(slab_total, each, blocks), "slab", 0, 0, tiled=True
    )
    spots = lax.all_gather(ordered[count : count + 2], "slab", axis=0)
    spots = spots.astype(jnp.int32)
    kz_all = spots[:, 0:1]
    ky_all = spots[:, 1:2]

    chunk = math.gcd(blocks, 256)
    span = math.gcd(depth, 32)
    width = math.gcd(blocks, 1024)
    per_row = blocks // width
    by_chunk = kz_all.reshape(slab_total * blocks // chunk, chunk)
    low = jnp.min(by_chunk, axis=1) // span
    high = jnp.max(by_chunk, axis=1) // span + 1
    ytab, ztab = right_table(freq), left_table(depth)
    pairs = each // 2
    imaged = pl.pallas_call(
        functools.partial(add_kernel, chunk, span),
        grid_spec=pltpu.PrefetchScalarGridSpec(
            num_scalar_prefetch=2,
            grid=(slab_total * per_row,),
            in_specs=[
                pl.BlockSpec((1, each, width), lambda i, a, b: (i // per_row, 0, i % per_row)),
                pl.BlockSpec((1, 1, width), lambda i, a, b: (i // per_row, 0, i % per_row)),
                pl.BlockSpec((1, 1, width), lambda i, a, b: (i // per_row, 0, i % per_row)),
                pl.BlockSpec(ytab.shape, lambda i, a, b: (0, 0)),
                pl.BlockSpec(ztab.shape, lambda i, a, b: (0, 0)),
            ],
            out_specs=pl.BlockSpec((pairs, depth, 2 * freq), lambda i, a, b: (0, 0, 0)),
            scratch_shapes=[pltpu.VMEM((each, depth, freq), jnp.float32)],
        ),
        out_shape=jax.ShapeDtypeStruct((pairs, depth, 2 * freq), jnp.bfloat16),
        name="add_yz",
    )(low, high, sent, kz_all, ky_all, ytab, ztab)

    split = imaged.reshape(pairs, slab_total, planes, 2 * freq)
    split = lax.all_to_all(jnp.swapaxes(split, 0, 1), "slab", 0, 0, tiled=True)
    split = split.reshape(slab_total, coils, x_here, planes, 2 * freq)
    split = jnp.transpose(split, (0, 2, 1, 3, 4)).reshape(
        coil_total, rows_out // coil_total, coils, planes, 2 * freq
    )
    split = lax.all_to_all(split, "coil", 0, 0, tiled=True)
    mine = jnp.transpose(split, (0, 2, 3, 1, 4)).reshape(sensitivity.shape).astype(jnp.float32)
    maps = sensitivity.astype(jnp.float32)
    map_re, map_im = maps[..., :freq], maps[..., freq:]
    img_re, img_im = mine[..., :freq], mine[..., freq:]
    real_part = jnp.sum(map_re * img_re + map_im * img_im, axis=0)
    imag_part = jnp.sum(map_re * img_im - map_im * img_re, axis=0)
    return jnp.concatenate([real_part, imag_part], axis=-1)


def solution(mesh):
    return jax.shard_map(
        per_device,
        mesh=mesh,
        in_specs=(
            P("coil", "slab", None),
            P("slab", None),
            P("slab"),
            P("slab"),
            P("slab", None),
            P(None, "slab", "coil", None),
        ),
        out_specs=P("slab", "coil", None),
        check_vma=False,
    )
```

time: 848 us -> 368 us (0.43); the launches traced: 837 us -> 367 us
  Pallas kernels: 0 us -> 257 us
  matrix products: 256 us -> 0 us
  waiting for transfers between devices: 238 us -> 23.6 us
  local copies, waits for them, and re-layouts: 169 us -> 20.8 us
  other arithmetic: 148 us -> 19.6 us
  blocking collectives: 0 us -> 36 us
  between operations: 15.3 us -> 0.15 us
    pallas_call x0 -> x3, Pallas kernels: none -> 257 us  [the longest x1 125 us: per_device(): pl.pallas_call(functools.partial(add_kernel, chunk, span), grid_spec=pltp...]
    dot_general x11 -> x0, matrix products: 256 us -> none  [the longest x8 233 us: one_group(): jnp.einsum('mij,mcpi->mcpj', weights, shaped, preferred_element_type=jnp....]
    scatter-add x1 -> x0, other arithmetic: 114 us -> none  [per_device(): kspace = jnp.zeros((grid_rows, cell_rows.shape[2]), jnp.float32).at[segme...]
    unnamed x4 -> x0, waiting for transfers between devices: 101 us -> none
    all_to_all x2, waiting for transfers between devices: 115 us -> 23.6 us  [the longest x1 23.6 us: per_device(): split = lax.all_to_all(split, 'coil', 0, 0, tiled=True)]
    scatter x2 -> x0, local copies, waits for them, and re-layouts: 73 us -> none  [pack_rows(): buffer = jnp.zeros((slab_total * capacity,) + member.shape[1:], member.dt...]
    convert_element_type x10 -> x5, other arithmetic: 25.8 us -> 2.12 us  [the longest x1 1.53 us: per_device(): maps = sensitivity.astype(jnp.float32)]
    reshape x11 -> x6, local copies, waits for them, and re-layouts: 30.6 us -> 7.28 us  [the longest x2 3.22 us: per_device(): lines = spread.reshape(coils, 2, slab_total, x_here, blocks)]
  transfers between devices with their start and end apart: 5 -> 2, of which waited for: 3 -> 1; matrix products, arithmetic and copies ran while one was open for 63% -> 2% of each run, Pallas kernels for 0% -> 0%
where the time goes in v1:
time: 368 us; the launch traced here: 367 us
  Pallas kernels  257 us (70%)
  blocking collectives  36 us (10%)
  waiting for transfers between devices  23.6 us (6%)
  local copies, waits for them, and re-layouts  20.8 us (6%)
  other arithmetic  19.6 us (5%)
  starting transfers between devices  10.1 us (3%)
    pallas_call x1, Pallas kernels, per_device(): pl.pallas_call(functools.partial(add_kernel, chunk, span), grid_spec=pltp...  125 us
    pallas_call x1, Pallas kernels, per_device(): pl.pallas_call(functools.partial(grid_kernel, stacked, coils, rows_out),...  116 us
    all_to_all x1, waiting for transfers between devices, per_device(): split = lax.all_to_all(split, 'coil', 0, 0, tiled=True)  23.6 us
    all_gather x1, blocking collectives, per_device(): spots = lax.all_gather(ordered[count:count + 2], 'slab', axis=0)  18.1 us
    all_to_all x1, blocking collectives, per_device(): split = lax.all_to_all(jnp.swapaxes(split, 0, 1), 'slab', 0, 0, tiled=True)  17.9 us
    pallas_call x1, Pallas kernels, per_device(): pl.pallas_call(sort_kernel, grid=(groups,), in_specs=[pl.BlockSpec((lines...  16.2 us
    unnamed x9, local copies, waits for them, and re-layouts  9.03 us
    reduce_sum x1, other arithmetic, per_device(): jnp.sum((key[:, :, None] < key[:, None, :]).astype(jnp.int32), axis=1)  8.06 us
  transfers between devices with their start and end apart: 2, of which 1 were waited for; matrix products, arithmetic and copies ran while one was open for 2% of the time, Pallas kernels for 0%

profile of v1, /device:TPU:0, one launch (start us, length us, event | category | flops | bytes accessed | tf_op | source)
XLA Modules:
  0.0 367.3 jit_solution(13860945055662390714)
XLA Ops:
  0.0 0.8 broadcast_multiply_fusion
  0.8 1.4 fusion.17
  2.3 0.1 cosine_multiply_fusion
  2.4 0.1 multiply_convert_fusion.1
  2.5 0.8 convert_element_type.70.tab_ref
  3.3 0.0 copy-start.1
  3.3 0.0 copy-start.2
  3.3 6.5 %copy.25 = bf16[2,8192,128]{1,2,0:T(8,128)(2,1)} copy(bf16[2,8192,128]{2,1,0:T(8,128)(2,1)} %param.6) | data formatting | bytes 8388608 | tf_op args[0]
  9.8 0.0 copy-done.1
  9.8 0.0 copy-done.2
  9.8 1.6 fusion.pos_ref
  11.4 116.1 %grid_x.1 = bf16[4,16,8192]{2,1,0:T(8,128)(2,1)} custom-call(f32[64,8192]{1,0:T(8,128)} %fusion.pos_ref, bf16[2,128,8192]{2,1,0:T(8,128)(2,1)} %bitcast.28, s32[1,8192]{1,0:T(1,128)} %bitcast.34, bf16[128,256]{1,0:T(8,128)(2,1)} %convert_element_type.70.tab_ref), custom_call_target="tpu_custom_call" | custom-call | tf_op jit(solution)/shard_map/grid_x/pallas_call | solution.py:176
  127.5 1.7 reshape.51
  129.2 1.5 copy.36
  130.7 0.4 reshape.52
  131.2 8.1 %convert_reduce_fusion = s32[4,2048]{1,0:T(4,128)S(1)} fusion(s32[4,2048]{1,0:T(4,128)S(1)} %lt.79), kind=kLoop, calls=%fused_computation | loop fusion | flops 50323456 | bytes 65536 | tf_op jit(solution)/shard_map/reduce_sum | solution.py:194
  139.2 0.6 copy.31
  139.9 0.1 fusion.8
  140.0 1.2 pad_maximum_fusion.vals_ref
  141.2 16.2 %order_kz.1 = bf16[80,8192]{1,0:T(8,128)(2,1)} custom-call(bf16[80,8192]{1,0:T(8,128)(2,1)} %pad_maximum_fusion.vals_ref, s32[1,8192]{1,0:T(1,128)} %bitcast.36), custom_call_target="tpu_custom_call" | custom-call | tf_op jit(solution)/shard_map/order_kz/pallas_call | solution.py:200
  157.3 2.3 slice_bitcast_fusion
  159.6 5.2 %all-to-all-start = ((bf16[8,8,8192]{2,1,0:T(8,128)(2,1)}), bf16[8,8,8192]{2,1,0:T(8,128)(2,1)S(1)}, u32[]{:S(2)}, u32[]{:S(2)}) async-start(bf16[8,8,8192]{2,1,0:T(8,128)(2,1)} %slice_bitcast_fusion), calls=%async_computation | async-start | bytes 2097152 | tf_op jit(solution)/shard_map/all_to_all | solution.py:213
  164.8 0.9 slice_bitcast_fusion.1
  165.8 18.1 %all-gather.1 = bf16[8,2,8192]{2,1,0:T(2,128)(2,1)S(1)} all-gather(bf16[1,2,8192]{2,1,0:T(2,128)(2,1)S(1)} %slice_bitcast_fusion.1), channel_id=2, replica_groups=mesh['slab'=8,'coil'=4] {'slab'}, dimensions={0}, use_global_device_ids=true | all-gather | bytes 294912 | tf_op jit(solution)/shard_map/all_gather | solution.py:216
  183.9 0.2 convert_element_type.81
  184.1 1.4 fusion.33
  185.6 1.0 fusion.12
  186.6 1.1 negate_convert_fusion
  187.7 0.1 fusion.32
  187.8 1.0 fusion.2
  188.9 0.6 and_select_fusion.1
  189.5 0.0 all-to-all-done.vals_ref
  189.5 0.0 copy-start
  189.5 1.0 copy-done
  190.5 124.8 %add_yz.1 = bf16[4,256,512]{2,1,0:T(8,128)(2,1)} custom-call(s32[256]{0:T(256)} %get-tuple-element.20.lo_ref, s32[256]{0:T(256)} %get-tuple-element.21.hi_ref, bf16[8,8,8192]{2,1,0:T(8,128)(2,1)} %copy-done, s32[8,1,8192]{2,1,0:T(1,128)} %get-tuple-element.11.kz_ref, s32[8,1,8192]{2,1,0:T(1,128)} %get-tuple-element.9.ky_ref, ...), custom_call_target="tpu_custom_call" | custom-call | tf_op jit(solution)/shard_map/add_yz/pallas_call | solution.py:230
  315.3 1.3 copy.35
  316.6 17.9 %all_to_all.15 = bf16[8,4,32,512]{3,2,1,0:T(8,128)(2,1)S(1)} all-to-all(bf16[8,4,32,512]{3,2,1,0:T(8,128)(2,1)S(1)} %bitcast.32), channel_id=1, replica_groups=mesh['slab'=8,'coil'=4] {'slab'}, dimensions={0} | all-to-all | bytes 2097152 | tf_op jit(solution)/shard_map/all_to_all | solution.py:250
  334.4 1.1 copy.28
  335.5 4.9 %all-to-all-start.2 = ((bf16[4,4,2,32,512]{4,3,2,1,0:T(8,128)(2,1)}), bf16[4,4,2,32,512]{4,3,2,1,0:T(8,128)(2,1)S(1)}, u32[]{:S(2)}, u32[]{:S(2)}) async-start(bf16[4,4,2,32,512]{4,3,2,1,0:T(8,128)(2,1)} %bitcast.11), calls=%async_computation.2 | async-start | bytes 2097152 | tf_op jit(solution)/shard_map/all_to_all | solution.py:255
  340.4 1.5 copy_convert_fusion
  341.9 23.6 %all-to-all-done.2 = bf16[4,4,2,32,512]{4,3,2,1,0:T(8,128)(2,1)S(1)} async-done(((bf16[4,4,2,32,512]{4,3,2,1,0:T(8,128)(2,1)}), bf16[4,4,2,32,512]{4,3,2,1,0:T(8,128)(2,1)S(1)}, u32[]{:S(2)}, u32[]{:S(2)}) %all-to-all-start.2) | async-done | bytes 1048608 | tf_op jit(solution)/shard_map/all_to_all | solution.py:255
  365.5 0.3 convert_bitcast_fusion
  365.8 0.3 copy.29
  366.1 0.3 add_reduce_fusion
  366.4 0.9 copy.30
  (8 shorter events, 0.1 us)
Async XLA Ops:
  3.3 6.5 %copy-start.1 = (bf16[8192,64]{0,1:T(8,128)(2,1)S(1)}, bf16[8192,64]{0,1:T(8,128)(2,1)}, u32[]{:S(2)}) copy-start(bf16[8192,64]{0,1:T(8,128)(2,1)} %param.7) | copy-start | bytes 3145732
  3.3 6.5 %copy-start.2 = (s32[8192]{0:T(1024)S(1)}, s32[8192]{0:T(1024)}, u32[]{:S(2)}) copy-start(s32[8192]{0:T(1024)} %param.8) | copy-start | bytes 98308
  159.6 29.9 %all-to-all-start = ((bf16[8,8,8192]{2,1,0:T(8,128)(2,1)}), bf16[8,8,8192]{2,1,0:T(8,128)(2,1)S(1)}, u32[]{:S(2)}, u32[]{:S(2)}) async-start(bf16[8,8,8192]{2,1,0:T(8,128)(2,1)} %slice_bitcast_fusion), calls=%async_computation | async-start | bytes 2097152 | tf_op jit(solution)/shard_map/all_to_all | solution.py:213
  189.5 1.0 copy-start
  335.5 30.0 %all-to-all-start.2 = ((bf16[4,4,2,32,512]{4,3,2,1,0:T(8,128)(2,1)}), bf16[4,4,2,32,512]{4,3,2,1,0:T(8,128)(2,1)S(1)}, u32[]{:S(2)}, u32[]{:S(2)}) async-start(bf16[4,4,2,32,512]{4,3,2,1,0:T(8,128)(2,1)} %bitcast.11), calls=%async_computation.2 | async-start | bytes 2097152 | tf_op jit(solution)/shard_map/all_to_all | solution.py:255

commit v2 on v1

--- a/solution.py
+++ b/solution.py
@@ -23,13 +23,10 @@
     return jnp.arange(count, dtype=jnp.int32)
 
 
-def across_stack(rows_out, stacked):
+def across_table(rows_out):
     x0 = (KX - rows_out) // 2
     cosine, sine = twiddle(x0 + ints(rows_out)[:, None], ints(CELLS)[None, :], KX)
-    table = jnp.concatenate([cosine, sine], axis=0)
-    eye = jnp.eye(stacked, dtype=jnp.float32)
-    full = eye[:, None, :, None] * table[None, :, None, :]
-    return full.reshape(stacked * 2 * rows_out, stacked * CELLS).astype(jnp.bfloat16)
+    return jnp.concatenate([cosine, sine], axis=0).astype(jnp.bfloat16)
 
 
 def right_table(length):
@@ -46,44 +43,41 @@
     return jnp.concatenate([upper, lower], axis=0).astype(jnp.bfloat16)
 
 
-def grid_kernel(stacked, coils, rows_out, pos_ref, val_ref, seg_ref, tab_ref, out_ref, wide):
-    lanes = pos_ref.shape[1]
-    wide[...] = val_ref[...].astype(jnp.float32)
+def grid_kernel(coils, rows_out, pos_ref, val_ref, seg_ref, tab_ref, out_ref, wide, where):
+    lanes = wide.shape[2]
     mid = (lax.broadcasted_iota(jnp.int32, (CELLS, lanes), 0).astype(jnp.float32) + 0.5) * 0.4
-    table = tab_ref[...]
-
-    def step(at, sums):
-        parts = []
-        for k in range(stacked):
-            offset = pos_ref[pl.ds(at * stacked + k, 1), :] - mid
+    x_at = lax.broadcasted_iota(jnp.int32, (rows_out, lanes), 0) + (KX - rows_out) // 2
+
+    @pl.loop(0, pos_ref.shape[1] // lanes)
+    def _(at):
+        cut = pl.ds(pl.multiple_of(at * lanes, lanes), lanes)
+        wide[...] = val_ref[:, :, cut].astype(jnp.float32)
+        where[...] = pos_ref[:, cut]
+
+        def step(i, sums):
+            offset = where[pl.ds(i, 1), :] - mid
             bump = jnp.maximum(1.0 - offset * offset, 0.0)
-            parts.append((bump * bump).astype(jnp.bfloat16))
-        moved = jnp.dot(
-            table, jnp.concatenate(parts, axis=0), preferred_element_type=jnp.float32
-        )
-        sums = list(sums)
-        for k in range(stacked):
-            base = k * 2 * rows_out
-            cosine = moved[base : base + rows_out]
-            sine = moved[base + rows_out : base + 2 * rows_out]
-            for c in range(coils):
-                re = wide[c, pl.ds(at * stacked + k, 1), :]
-                im = wide[c, pl.ds(CELLS + at * stacked + k, 1), :]
-                sums[2 * c] = sums[2 * c] + (re * cosine - im * sine)
-                sums[2 * c + 1] = sums[2 * c + 1] + (re * sine + im * cosine)
-        return tuple(sums)
-
-    zero = jnp.zeros((rows_out, lanes), jnp.float32)
-    sums = lax.fori_loop(0, CELLS // stacked, step, (zero,) * (2 * coils))
-    x_at = lax.broadcasted_iota(jnp.int32, (rows_out, lanes), 0) + (KX - rows_out) // 2
-    turn = (x_at * seg_ref[...]) & 3
-    for c in range(coils):
-        re, im = sums[2 * c], sums[2 * c + 1]
-        new_re = jnp.where((turn & 1) == 0, re, -im)
-        new_im = jnp.where((turn & 1) == 0, im, re)
+            weight = (bump * bump).astype(jnp.bfloat16).astype(jnp.float32)
+            return tuple(
+                sums[n] + weight * wide[n // 2, pl.ds(n % 2 * CELLS + i, 1), :]
+                for n in range(2 * coils)
+            )
+
+        zero = jnp.zeros((CELLS, lanes), jnp.float32)
+        sums = lax.fori_loop(0, CELLS, step, (zero,) * (2 * coils), unroll=4)
+        turn = (x_at * seg_ref[:, cut]) & 3
         sign = jnp.where(turn >= 2, -1.0, 1.0)
-        out_ref[2 * c] = (new_re * sign).astype(jnp.bfloat16)
-        out_ref[2 * c + 1] = (new_im * sign).astype(jnp.bfloat16)
+        cells = jnp.concatenate([part.astype(jnp.bfloat16) for part in sums], axis=1)
+        moved = jnp.dot(tab_ref[...], cells, preferred_element_type=jnp.float32)
+        for c in range(coils):
+            of_re = moved[:, 2 * c * lanes : (2 * c + 1) * lanes]
+            of_im = moved[:, (2 * c + 1) * lanes : (2 * c + 2) * lanes]
+            re = of_re[:rows_out] - of_im[rows_out:]
+            im = of_re[rows_out:] + of_im[:rows_out]
+            new_re = jnp.where((turn & 1) == 0, re, -im)
+            new_im = jnp.where((turn & 1) == 0, im, re)
+            out_ref[2 * c, :, cut] = (new_re * sign).astype(jnp.bfloat16)
+            out_ref[2 * c + 1, :, cut] = (new_im * sign).astype(jnp.bfloat16)
 
 
 def sort_kernel(vals_ref, rank_ref, out_ref):
@@ -100,44 +94,53 @@
 
 
 def add_kernel(
-    chunk, span, lo_ref, hi_ref, vals_ref, kz_ref, ky_ref, ytab_ref, ztab_ref, out_ref, total
+    chunk, span, lo_ref, more_ref, vals_ref, kz_ref, ky_ref, ytab_ref, ztab_ref, out_ref, total
 ):
     step = pl.program_id(0)
     rows = vals_ref.shape[1]
     width = vals_ref.shape[2]
-    depth, freq = total.shape[1], total.shape[2]
+    depth, freq = out_ref.shape[1], total.shape[2]
+    parts = width // chunk
+    spot = lax.broadcasted_iota(jnp.int32, (freq, chunk), 0)
+    plane = lax.broadcasted_iota(jnp.int32, (span, chunk), 0)
 
     @pl.when(step == 0)
     def _():
         total[...] = jnp.zeros_like(total)
 
-    for part in range(width // chunk):
+    def add(part, start):
         cut = slice(part * chunk, (part + 1) * chunk)
-        spot = lax.broadcasted_iota(jnp.int32, (freq, chunk), 0)
         hot = jnp.where(spot == ky_ref[0, :, cut], 1.0, 0.0).astype(jnp.bfloat16)
-        plane = lax.broadcasted_iota(jnp.int32, (span, chunk), 0)
-        kz = kz_ref[0, :, cut]
-        vals = [vals_ref[0, v : v + 1, cut].astype(jnp.float32) for v in range(rows)]
-        at_chunk = step * (width // chunk) + part
-
-        def one(at, carry):
-            start = pl.multiple_of(at * span, span)
-            mine = plane == (kz - start)
-            left = jnp.concatenate(
-                [jnp.where(mine, vals[v], 0.0).astype(jnp.bfloat16) for v in range(rows)], axis=0
-            )
-            moved = lax.dot_general(left, hot, NT, preferred_element_type=jnp.float32)
-            for v in range(rows):
-                total[v, pl.ds(start, span), :] += moved[v * span : (v + 1) * span]
+        mine = jnp.where(plane == (kz_ref[0, :, cut] - start), 1.0, 0.0).astype(jnp.bfloat16)
+        left = []
+        for v in range(rows):
+            row = vals_ref[0, v : v + 1, cut].astype(jnp.float32)
+            row = jnp.broadcast_to(row, (16, chunk)).astype(jnp.bfloat16)
+            left.append(mine * jnp.concatenate([row] * (span // 16), axis=0))
+        left = jnp.concatenate(left, axis=0)
+        moved = lax.dot_general(left, hot, NT, preferred_element_type=jnp.float32)
+        for v in range(rows):
+            total[v, pl.ds(start, span), :] += moved[v * span : (v + 1) * span]
+
+    for part in range(parts):
+        add(part, pl.multiple_of(lo_ref[step * parts + part], 8))
+
+    for part in range(parts):
+        first = lo_ref[step * parts + part]
+
+        def again(at, carry):
+            add(part, pl.multiple_of(first + at * span, 8))
             return carry
 
-        lax.fori_loop(lo_ref[at_chunk], hi_ref[at_chunk], one, 0)
+        lax.fori_loop(1, more_ref[step * parts + part], again, 0)
 
     @pl.when(step == pl.num_programs(0) - 1)
     def _():
         pairs = rows // 2
         for pair in range(pairs):
-            both = jnp.concatenate([total[2 * pair], total[2 * pair + 1]], axis=1)
+            both = jnp.concatenate(
+                [total[2 * pair, :depth, :], total[2 * pair + 1, :depth, :]], axis=1
+            )
             planes = jnp.dot(
                 both.astype(jnp.bfloat16), ytab_ref[...], preferred_element_type=jnp.float32
             ).astype(jnp.bfloat16)
@@ -170,11 +173,10 @@
     kz = block_slab[:, 0] * planes + grid_block // (segments * freq)
     ky = grid_block // segments % freq
 
-    stacked = 4
-    tile = math.gcd(blocks, 256)
-    table = across_stack(rows_out, stacked)
+    tile = math.gcd(blocks, 1024)
+    table = across_table(rows_out)
     spread = pl.pallas_call(
-        functools.partial(grid_kernel, stacked, coils, rows_out),
+        functools.partial(grid_kernel, coils, rows_out),
         grid=(blocks // tile,),
         in_specs=[
             pl.BlockSpec((CELLS, tile), lambda b: (0, b)),
@@ -184,7 +186,10 @@
         ],
         out_specs=pl.BlockSpec((2 * coils, rows_out, tile), lambda b: (0, 0, b)),
         out_shape=jax.ShapeDtypeStruct((2 * coils, rows_out, blocks), jnp.bfloat16),
-        scratch_shapes=[pltpu.VMEM((coils, 2 * CELLS, tile), jnp.float32)],
+        scratch_shapes=[
+            pltpu.VMEM((coils, 2 * CELLS, math.gcd(tile, 128)), jnp.float32),
+            pltpu.VMEM((CELLS, math.gcd(tile, 128)), jnp.float32),
+        ],
         name="grid_x",
     )(pos, vals, seg, table)
 
@@ -213,18 +218,18 @@
     sent = lax.all_to_all(
         ordered[:count].reshape(slab_total, each, blocks), "slab", 0, 0, tiled=True
     )
-    spots = lax.all_gather(ordered[count : count + 2], "slab", axis=0)
-    spots = spots.astype(jnp.int32)
+    spots = jnp.broadcast_to(ordered[count : count + 2][None], (slab_total, 2, blocks))
+    spots = lax.all_to_all(spots, "slab", 0, 0, tiled=True).astype(jnp.int32)
     kz_all = spots[:, 0:1]
     ky_all = spots[:, 1:2]
 
     chunk = math.gcd(blocks, 256)
-    span = math.gcd(depth, 32)
+    span = 64
     width = math.gcd(blocks, 1024)
     per_row = blocks // width
     by_chunk = kz_all.reshape(slab_total * blocks // chunk, chunk)
-    low = jnp.min(by_chunk, axis=1) // span
-    high = jnp.max(by_chunk, axis=1) // span + 1
+    low = jnp.min(by_chunk, axis=1) // 8 * 8
+    high = (jnp.max(by_chunk, axis=1) - low) // span + 1
     ytab, ztab = right_table(freq), left_table(depth)
     pairs = each // 2
     imaged = pl.pallas_call(
@@ -240,7 +245,7 @@
                 pl.BlockSpec(ztab.shape, lambda i, a, b: (0, 0)),
             ],
             out_specs=pl.BlockSpec((pairs, depth, 2 * freq), lambda i, a, b: (0, 0, 0)),
-            scratch_shapes=[pltpu.VMEM((each, depth, freq), jnp.float32)],
+            scratch_shapes=[pltpu.VMEM((each, depth + span, freq), jnp.float32)],
         ),
         out_shape=jax.ShapeDtypeStruct((pairs, depth, 2 * freq), jnp.bfloat16),
         name="add_yz",

time: 368 us -> 266 us (0.72)
  Pallas kernels: 257 us -> 153 us
  blocking collectives: 36 us -> 17.8 us
  waiting for transfers between devices: 23.6 us -> 37.9 us
    pallas_call x1, Pallas kernels: 125 us -> 49.7 us  [per_device(): pl.pallas_call(functools.partial(add_kernel, chunk, span), grid_spec=pltp...]
    pallas_call x1, Pallas kernels: 116 us -> 86.8 us  [per_device(): pl.pallas_call(functools.partial(grid_kernel, coils, rows_out), grid=(blo...]
    all_gather x1 -> x0, blocking collectives: 18.1 us -> none  [per_device(): spots = lax.all_gather(ordered[count:count + 2], 'slab', axis=0)]
    all_to_all x1, waiting for transfers between devices: 0.01 us -> 9.69 us  [per_device(): lax.all_to_all(ordered[:count].reshape(slab_total, each, blocks), 'slab',...]
    all_to_all x0 -> x1, starting transfers between devices: none -> 5.2 us  [per_device(): spots = lax.all_to_all(spots, 'slab', 0, 0, tiled=True).astype(jnp.int32)]
    all_to_all x0 -> x1, waiting for transfers between devices: none -> 4.62 us  [per_device(): spots = lax.all_to_all(spots, 'slab', 0, 0, tiled=True).astype(jnp.int32)]
    unnamed x9 -> x8, local copies, waits for them, and re-layouts: 9.03 us -> 8.11 us
  transfers between devices with their start and end apart: 2 -> 3, of which waited for: 1 -> 3; matrix products, arithmetic and copies ran while one was open for 2% -> 4% of each run, Pallas kernels for 0% -> 0%
where the time goes in v2:
time: 266 us; the launch traced here: 263 us
  Pallas kernels  153 us (58%)
  waiting for transfers between devices  37.9 us (14%)
  local copies, waits for them, and re-layouts  20.9 us (8%)
  other arithmetic  20.1 us (8%)
  blocking collectives  17.8 us (7%)
  starting transfers between devices  13.6 us (5%)
    pallas_call x1, Pallas kernels, per_device(): pl.pallas_call(functools.partial(grid_kernel, coils, rows_out), grid=(blo...  86.8 us
    pallas_call x1, Pallas kernels, per_device(): pl.pallas_call(functools.partial(add_kernel, chunk, span), grid_spec=pltp...  49.7 us
    all_to_all x1, waiting for transfers between devices, per_device(): split = lax.all_to_all(split, 'coil', 0, 0, tiled=True)  23.6 us
    all_to_all x1, blocking collectives, per_device(): split = lax.all_to_all(jnp.swapaxes(split, 0, 1), 'slab', 0, 0, tiled=True)  17.8 us
    pallas_call x1, Pallas kernels, per_device(): pl.pallas_call(sort_kernel, grid=(groups,), in_specs=[pl.BlockSpec((lines...  16.2 us
    all_to_all x1, waiting for transfers between devices, per_device(): lax.all_to_all(ordered[:count].reshape(slab_total, each, blocks), 'slab',...  9.69 us
    unnamed x8, local copies, waits for them, and re-layouts  8.11 us
    reduce_sum x1, other arithmetic, per_device(): jnp.sum((key[:, :, None] < key[:, None, :]).astype(jnp.int32), axis=1)  8.06 us
  transfers between devices with their start and end apart: 3, of which 3 were waited for; matrix products, arithmetic and copies ran while one was open for 4% of the time, Pallas kernels for 0%

profile of v2, /device:TPU:0, one launch (start us, length us, event | category | flops | bytes accessed | tf_op | source)
XLA Modules:
  0.0 263.2 jit_solution(3411845001896227295)
XLA Ops:
  0.0 0.8 broadcast_multiply_fusion
  0.8 1.4 fusion.17
  2.3 0.1 multiply_convert_fusion.2
  2.4 0.0 copy-start.1
  2.4 0.0 copy-start.2
  2.4 6.5 %copy.25 = bf16[2,8192,128]{1,2,0:T(8,128)(2,1)} copy(bf16[2,8192,128]{2,1,0:T(8,128)(2,1)} %param.6) | data formatting | bytes 8388608 | tf_op args[0]
  8.9 0.6 pad_maximum_fusion.6.tab_ref
  9.5 0.0 copy-done.1
  9.5 0.0 copy-done.2
  9.5 1.6 fusion.pos_ref
  11.1 86.8 %grid_x.1 = bf16[4,16,8192]{2,1,0:T(8,128)(2,1)} custom-call(f32[64,8192]{1,0:T(8,128)} %fusion.pos_ref, bf16[2,128,8192]{2,1,0:T(8,128)(2,1)} %bitcast.26, s32[1,8192]{1,0:T(1,128)} %bitcast.32, bf16[32,64]{1,0:T(8,128)(2,1)} %pad_maximum_fusion.6.tab_ref), custom_call_target="tpu_custom_call" | custom-call | tf_op jit(solution)/shard_map/grid_x/pallas_call | solution.py:178
  97.9 1.7 reshape.38
  99.7 1.5 copy.36
  101.1 0.4 reshape.39
  101.6 8.1 %convert_reduce_fusion = s32[4,2048]{1,0:T(4,128)S(1)} fusion(s32[4,2048]{1,0:T(4,128)S(1)} %lt.79), kind=kLoop, calls=%fused_computation | loop fusion | flops 50323456 | bytes 65536 | tf_op jit(solution)/shard_map/reduce_sum | solution.py:199
  109.7 0.6 copy.31
  110.3 0.1 fusion.8
  110.4 1.2 pad_maximum_fusion.vals_ref
  111.6 16.2 %order_kz.1 = bf16[80,8192]{1,0:T(8,128)(2,1)} custom-call(bf16[80,8192]{1,0:T(8,128)(2,1)} %pad_maximum_fusion.vals_ref, s32[1,8192]{1,0:T(1,128)} %bitcast.34), custom_call_target="tpu_custom_call" | custom-call | tf_op jit(solution)/shard_map/order_kz/pallas_call | solution.py:205
  127.8 0.9 slice.33
  128.7 0.8 broadcast_in_dim.10
  129.5 5.2 %all-to-all-start = ((bf16[8,2,8192]{2,1,0:T(2,128)(2,1)}), bf16[8,2,8192]{2,1,0:T(2,128)(2,1)S(1)}, u32[]{:S(2)}, u32[]{:S(2)}) async-start(bf16[8,2,8192]{2,1,0:T(2,128)(2,1)} %broadcast_in_dim.10), calls=%async_computation | async-start | bytes 524288 | tf_op jit(solution)/shard_map/all_to_all | solution.py:222
  134.7 2.3 slice_bitcast_fusion
  137.0 4.6 %all-to-all-done = bf16[8,2,8192]{2,1,0:T(2,128)(2,1)S(1)} async-done(((bf16[8,2,8192]{2,1,0:T(2,128)(2,1)}), bf16[8,2,8192]{2,1,0:T(2,128)(2,1)S(1)}, u32[]{:S(2)}, u32[]{:S(2)}) %all-to-all-start) | async-done | bytes 262176 | tf_op jit(solution)/shard_map/all_to_all | solution.py:222
  141.6 3.6 %all-to-all-start.1 = ((bf16[8,8,8192]{2,1,0:T(8,128)(2,1)}), bf16[8,8,8192]{2,1,0:T(8,128)(2,1)S(1)}, u32[]{:S(2)}, u32[]{:S(2)}) async-start(bf16[8,8,8192]{2,1,0:T(8,128)(2,1)} %slice_bitcast_fusion), calls=%async_computation.1 | async-start | bytes 2097152 | tf_op jit(solution)/shard_map/all_to_all | solution.py:218
  145.2 1.0 fusion.12
  146.2 1.1 negate_convert_fusion
  147.3 1.0 fusion.2
  148.4 0.2 convert_element_type.58
  148.6 1.4 fusion.34
  150.1 0.1 fusion.32
  150.2 0.6 fusion.29
  150.8 9.7 %all-to-all-done.1.vals_ref = bf16[8,8,8192]{2,1,0:T(8,128)(2,1)S(1)} async-done(((bf16[8,8,8192]{2,1,0:T(8,128)(2,1)}), bf16[8,8,8192]{2,1,0:T(8,128)(2,1)S(1)}, u32[]{:S(2)}, u32[]{:S(2)}) %all-to-all-start.1) | async-done | bytes 1048608 | tf_op jit(solution)/shard_map/all_to_all | solution.py:218
  160.5 0.0 copy-start
  160.5 1.0 copy-done
  161.5 49.7 %add_yz.1 = bf16[4,256,512]{2,1,0:T(8,128)(2,1)} custom-call(s32[256]{0:T(256)} %get-tuple-element.10.lo_ref, s32[256]{0:T(256)} %get-tuple-element.9.more_ref, bf16[8,8,8192]{2,1,0:T(8,128)(2,1)} %copy-done, s32[8,1,8192]{2,1,0:T(1,128)} %get-tuple-element.13.kz_ref, s32[8,1,8192]{2,1,0:T(1,128)} %get-tuple-element.11.ky_ref, ...), custom_call_target="tpu_custom_call" | custom-call | tf_op jit(solution)/shard_map/add_yz/pallas_call | solution.py:235
  211.2 1.3 copy.35
  212.5 17.8 %all_to_all.20 = bf16[8,4,32,512]{3,2,1,0:T(8,128)(2,1)S(1)} all-to-all(bf16[8,4,32,512]{3,2,1,0:T(8,128)(2,1)S(1)} %bitcast.30), channel_id=1, replica_groups=mesh['slab'=8,'coil'=4] {'slab'}, dimensions={0} | all-to-all | bytes 2097152 | tf_op jit(solution)/shard_map/all_to_all | solution.py:255
  230.3 1.1 copy.28
  231.4 4.9 %all-to-all-start.3 = ((bf16[4,4,2,32,512]{4,3,2,1,0:T(8,128)(2,1)}), bf16[4,4,2,32,512]{4,3,2,1,0:T(8,128)(2,1)S(1)}, u32[]{:S(2)}, u32[]{:S(2)}) async-start(bf16[4,4,2,32,512]{4,3,2,1,0:T(8,128)(2,1)} %bitcast.10), calls=%async_computation.3 | async-start | bytes 2097152 | tf_op jit(solution)/shard_map/all_to_all | solution.py:260
  236.2 1.5 copy_convert_fusion
  237.8 23.6 %all-to-all-done.3 = bf16[4,4,2,32,512]{4,3,2,1,0:T(8,128)(2,1)S(1)} async-done(((bf16[4,4,2,32,512]{4,3,2,1,0:T(8,128)(2,1)}), bf16[4,4,2,32,512]{4,3,2,1,0:T(8,128)(2,1)S(1)}, u32[]{:S(2)}, u32[]{:S(2)}) %all-to-all-start.3) | async-done | bytes 1048608 | tf_op jit(solution)/shard_map/all_to_all | solution.py:260
  261.4 0.3 convert_bitcast_fusion
  261.7 0.3 copy.29
  262.0 0.3 add_reduce_fusion
  262.3 0.9 copy.30
  (6 shorter events, 0.1 us)
Async XLA Ops:
  2.4 7.1 %copy-start.1 = (bf16[8192,64]{0,1:T(8,128)(2,1)S(1)}, bf16[8192,64]{0,1:T(8,128)(2,1)}, u32[]{:S(2)}) copy-start(bf16[8192,64]{0,1:T(8,128)(2,1)} %param.7) | copy-start | bytes 3145732
  2.4 7.1 %copy-start.2 = (s32[8192]{0:T(1024)S(1)}, s32[8192]{0:T(1024)}, u32[]{:S(2)}) copy-start(s32[8192]{0:T(1024)} %param.8) | copy-start | bytes 98308
  129.5 12.1 %all-to-all-start = ((bf16[8,2,8192]{2,1,0:T(2,128)(2,1)}), bf16[8,2,8192]{2,1,0:T(2,128)(2,1)S(1)}, u32[]{:S(2)}, u32[]{:S(2)}) async-start(bf16[8,2,8192]{2,1,0:T(2,128)(2,1)} %broadcast_in_dim.10), calls=%async_computation | async-start | bytes 524288 | tf_op jit(solution)/shard_map/all_to_all | solution.py:222
  141.6 18.9 %all-to-all-start.1 = ((bf16[8,8,8192]{2,1,0:T(8,128)(2,1)}), bf16[8,8,8192]{2,1,0:T(8,128)(2,1)S(1)}, u32[]{:S(2)}, u32[]{:S(2)}) async-start(bf16[8,8,8192]{2,1,0:T(8,128)(2,1)} %slice_bitcast_fusion), calls=%async_computation.1 | async-start | bytes 2097152 | tf_op jit(solution)/shard_map/all_to_all | solution.py:218
  160.5 1.0 copy-start
  231.4 30.0 %all-to-all-start.3 = ((bf16[4,4,2,32,512]{4,3,2,1,0:T(8,128)(2,1)}), bf16[4,4,2,32,512]{4,3,2,1,0:T(8,128)(2,1)S(1)}, u32[]{:S(2)}, u32[]{:S(2)}) async-start(bf16[4,4,2,32,512]{4,3,2,1,0:T(8,128)(2,1)} %bitcast.10), calls=%async_computation.3 | async-start | bytes 2097152 | tf_op jit(solution)/shard_map/all_to_all | solution.py:260

commit v3 on v2

--- a/solution.py
+++ b/solution.py
@@ -23,10 +23,18 @@
     return jnp.arange(count, dtype=jnp.int32)
 
 
-def across_table(rows_out):
+def across_table(coils, rows_out, x_here):
     x0 = (KX - rows_out) // 2
     cosine, sine = twiddle(x0 + ints(rows_out)[:, None], ints(CELLS)[None, :], KX)
-    return jnp.concatenate([cosine, sine], axis=0).astype(jnp.bfloat16)
+    upper = jnp.stack([cosine, -sine], axis=1)
+    lower = jnp.stack([sine, cosine], axis=1)
+    eye = jnp.eye(coils, dtype=jnp.float32)
+    tables = []
+    for one in (jnp.stack([upper, lower], axis=1), jnp.stack([-lower, upper], axis=1)):
+        one = one.reshape(rows_out // x_here, 1, x_here, 2, 1, 2, CELLS)
+        one = one * eye[None, :, None, None, :, None, None]
+        tables.append(one.reshape(2 * coils * rows_out, 2 * coils * CELLS))
+    return jnp.concatenate(tables, axis=0).astype(jnp.bfloat16)
 
 
 def right_table(length):
@@ -43,15 +51,16 @@
     return jnp.concatenate([upper, lower], axis=0).astype(jnp.bfloat16)
 
 
-def grid_kernel(coils, rows_out, pos_ref, val_ref, seg_ref, tab_ref, out_ref, wide, where):
+def grid_kernel(coils, pos_ref, val_ref, seg_ref, x_ref, tab_ref, out_ref, wide, where):
     lanes = wide.shape[2]
+    rows = out_ref.shape[0]
     mid = (lax.broadcasted_iota(jnp.int32, (CELLS, lanes), 0).astype(jnp.float32) + 0.5) * 0.4
-    x_at = lax.broadcasted_iota(jnp.int32, (rows_out, lanes), 0) + (KX - rows_out) // 2
 
     @pl.loop(0, pos_ref.shape[1] // lanes)
     def _(at):
         cut = pl.ds(pl.multiple_of(at * lanes, lanes), lanes)
-        wide[...] = val_ref[:, :, cut].astype(jnp.float32)
+        for c in range(coils):
+            wide[c] = val_ref[c, cut, :].astype(jnp.float32).T
         where[...] = pos_ref[:, cut]
 
         def step(i, sums):
@@ -65,32 +74,27 @@
 
         zero = jnp.zeros((CELLS, lanes), jnp.float32)
         sums = lax.fori_loop(0, CELLS, step, (zero,) * (2 * coils), unroll=4)
-        turn = (x_at * seg_ref[:, cut]) & 3
-        sign = jnp.where(turn >= 2, -1.0, 1.0)
-        cells = jnp.concatenate([part.astype(jnp.bfloat16) for part in sums], axis=1)
+        turn = (x_ref[...] * seg_ref[:, cut]) & 3
+        cells = jnp.concatenate([part.astype(jnp.bfloat16) for part in sums], axis=0)
         moved = jnp.dot(tab_ref[...], cells, preferred_element_type=jnp.float32)
-        for c in range(coils):
-            of_re = moved[:, 2 * c * lanes : (2 * c + 1) * lanes]
-            of_im = moved[:, (2 * c + 1) * lanes : (2 * c + 2) * lanes]
-            re = of_re[:rows_out] - of_im[rows_out:]
-            im = of_re[rows_out:] + of_im[:rows_out]
-            new_re = jnp.where((turn & 1) == 0, re, -im)
-            new_im = jnp.where((turn & 1) == 0, im, re)
-            out_ref[2 * c, :, cut] = (new_re * sign).astype(jnp.bfloat16)
-            out_ref[2 * c + 1, :, cut] = (new_im * sign).astype(jnp.bfloat16)
-
-
-def sort_kernel(vals_ref, rank_ref, out_ref):
-    group = vals_ref.shape[1]
-    tile = min(256, group)
+        turned = jnp.where((turn & 1) == 0, moved[:rows], moved[rows:])
+        out_ref[:, cut] = jnp.where(turn >= 2, -turned, turned).astype(jnp.bfloat16)
+
+
+def sort_kernel(vals_ref, spot_ref, rank_ref, out_ref, spot_out_ref):
+    rows, group = vals_ref.shape
+    tile = math.gcd(256, group)
+    slot = lax.broadcasted_iota(jnp.int32, (tile, group), 0)
+    vals = jnp.concatenate([vals_ref[...], spot_ref[...]], axis=0)
 
     @pl.loop(0, group // tile)
     def _(at):
         start = pl.multiple_of(at * tile, tile)
-        slot = lax.broadcasted_iota(jnp.int32, (tile, group), 0) + start
-        hot = jnp.where(slot == rank_ref[...], 1.0, 0.0).astype(jnp.bfloat16)
-        moved = lax.dot_general(vals_ref[...], hot, NT, preferred_element_type=jnp.float32)
-        out_ref[:, pl.ds(start, tile)] = moved.astype(jnp.bfloat16)
+        hot = jnp.where(slot == (rank_ref[...] - start), 1.0, 0.0).astype(jnp.bfloat16)
+        moved = lax.dot_general(vals, hot, NT, preferred_element_type=jnp.float32)
+        moved = moved.astype(jnp.bfloat16)
+        out_ref[:, pl.ds(start, tile)] = moved[:rows]
+        spot_out_ref[:, pl.ds(start, tile)] = moved[rows:]
 
 
 def add_kernel(
@@ -168,57 +172,64 @@
 
     live = ints(CELLS)[:, None] < block_count[None, :]
     pos = jnp.where(live, sample_pos.T.astype(jnp.float32), 1.0e4) * 0.4
-    vals = jnp.swapaxes(samples, 1, 2)
     seg = (grid_block % segments)[None, :]
     kz = block_slab[:, 0] * planes + grid_block // (segments * freq)
     ky = grid_block // segments % freq
 
     tile = math.gcd(blocks, 1024)
-    table = across_table(rows_out)
-    spread = pl.pallas_call(
-        functools.partial(grid_kernel, coils, rows_out),
+    lanes = math.gcd(tile, 128)
+    count = 2 * coils * rows_out
+    table = across_table(coils, rows_out, x_here)
+    x_at = (ints(count) // (2 * coils * x_here)) * x_here + ints(count) // 2 % x_here
+    x_at = jnp.broadcast_to((x_at + (KX - rows_out) // 2)[:, None], (count, lanes))
+    lines = pl.pallas_call(
+        functools.partial(grid_kernel, coils),
         grid=(blocks // tile,),
         in_specs=[
             pl.BlockSpec((CELLS, tile), lambda b: (0, b)),
-            pl.BlockSpec((coils, 2 * CELLS, tile), lambda b: (0, 0, b)),
+            pl.BlockSpec((coils, tile, 2 * CELLS), lambda b: (0, b, 0)),
             pl.BlockSpec((1, tile), lambda b: (0, b)),
+            pl.BlockSpec(x_at.shape, lambda b: (0, 0)),
             pl.BlockSpec(table.shape, lambda b: (0, 0)),
         ],
-        out_specs=pl.BlockSpec((2 * coils, rows_out, tile), lambda b: (0, 0, b)),
-        out_shape=jax.ShapeDtypeStruct((2 * coils, rows_out, blocks), jnp.bfloat16),
+        out_specs=pl.BlockSpec((count, tile), lambda b: (0, b)),
+        out_shape=jax.ShapeDtypeStruct((count, blocks), jnp.bfloat16),
         scratch_shapes=[
-            pltpu.VMEM((coils, 2 * CELLS, math.gcd(tile, 128)), jnp.float32),
-            pltpu.VMEM((CELLS, math.gcd(tile, 128)), jnp.float32),
+            pltpu.VMEM((coils, 2 * CELLS, lanes), jnp.float32),
+            pltpu.VMEM((CELLS, lanes), jnp.float32),
         ],
         name="grid_x",
-    )(pos, vals, seg, table)
+    )(pos, samples, seg, x_at, table)
 
     group = math.gcd(blocks, 2048)
     groups = blocks // group
     key = (kz * group + ints(blocks) % group).reshape(groups, group)
     rank = jnp.sum((key[:, :, None] < key[:, None, :]).astype(jnp.int32), axis=1)
     rank = rank.reshape(1, blocks)
-    lines = spread.reshape(coils, 2, slab_total, x_here, blocks)
-    lines = jnp.transpose(lines, (2, 0, 3, 1, 4)).reshape(2 * coils * rows_out, blocks)
-    spots = jnp.stack([kz, ky]).astype(jnp.bfloat16)
-    lines = jnp.concatenate([lines, jnp.pad(spots, ((0, 14), (0, 0)))], axis=0)
-    ordered = pl.pallas_call(
+    spots = jnp.pad(jnp.stack([kz, ky]).astype(jnp.bfloat16), ((0, 14), (0, 0)))
+    ordered, spots = pl.pallas_call(
         sort_kernel,
         grid=(groups,),
         in_specs=[
-            pl.BlockSpec((lines.shape[0], group), lambda b: (0, b)),
+            pl.BlockSpec((count, group), lambda b: (0, b)),
+            pl.BlockSpec((16, group), lambda b: (0, b)),
             pl.BlockSpec((1, group), lambda b: (0, b)),
         ],
-        out_specs=pl.BlockSpec((lines.shape[0], group), lambda b: (0, b)),
-        out_shape=jax.ShapeDtypeStruct(lines.shape, jnp.bfloat16),
+        out_specs=[
+            pl.BlockSpec((count, group), lambda b: (0, b)),
+            pl.BlockSpec((16, group), lambda b: (0, b)),
+        ],
+        out_shape=[
+            jax.ShapeDtypeStruct((count, blocks), jnp.bfloat16),
+            jax.ShapeDtypeStruct((16, blocks), jnp.bfloat16),
+        ],
         name="order_kz",
-    )(lines, rank)
-    count = 2 * coils * rows_out
+    )(lines, spots, rank)
     each = 2 * coils * x_here
     sent = lax.all_to_all(
-        ordered[:count].reshape(slab_total, each, blocks), "slab", 0, 0, tiled=True
+        ordered.reshape(slab_total, each, blocks), "slab", 0, 0, tiled=True
     )
-    spots = jnp.broadcast_to(ordered[count : count + 2][None], (slab_total, 2, blocks))
+    spots = jnp.broadcast_to(spots[:2][None], (slab_total, 2, blocks))
     spots = lax.all_to_all(spots, "slab", 0, 0, tiled=True).astype(jnp.int32)
     kz_all = spots[:, 0:1]
     ky_all = spots[:, 1:2]

time: 266 us -> 262 us (0.985)
  local copies, waits for them, and re-layouts: 20.9 us -> 8.71 us
  blocking collectives: 17.8 us -> 29.7 us
  starting transfers between devices: 13.6 us -> 8.43 us
  waiting for transfers between devices: 37.9 us -> 33.3 us
  Pallas kernels: 153 us -> 157 us
    all_to_all x0 -> x1, blocking collectives: none -> 11.9 us  [per_device(): spots = lax.all_to_all(spots, 'slab', 0, 0, tiled=True).astype(jnp.int32)]
    unnamed x8 -> x5, local copies, waits for them, and re-layouts: 8.11 us -> 1.64 us
    reshape x4 -> x0, local copies, waits for them, and re-layouts: 5.94 us -> none  [the longest x2 3.22 us: per_device(): lines = spread.reshape(coils, 2, slab_total, x_here, blocks)]
    all_to_all x2 -> x1, starting transfers between devices: 8.76 us -> 3.56 us  [per_device(): lax.all_to_all(ordered.reshape(slab_total, each, blocks), 'slab', 0, 0, t...]
    pallas_call x2, Pallas kernels: 103 us -> 108 us  [the longest x1 91.5 us: per_device(): pl.pallas_call(functools.partial(grid_kernel, coils), grid=(blocks // til...]
    all_to_all x2 -> x1, waiting for transfers between devices: 14.3 us -> 9.65 us  [per_device(): lax.all_to_all(ordered.reshape(slab_total, each, blocks), 'slab', 0, 0, t...]
  transfers between devices with their start and end apart: 3 -> 2, of which waited for: 3 -> 2; matrix products, arithmetic and copies ran while one was open for 4% -> 3% of each run, Pallas kernels for 0% -> 0%
where the time goes in v3:
time: 262 us; the launch traced here: 258 us
  Pallas kernels  157 us (60%)
  waiting for transfers between devices  33.3 us (13%)
  blocking collectives  29.7 us (11%)
  other arithmetic  20.8 us (8%)
  local copies, waits for them, and re-layouts  8.71 us (3%)
  starting transfers between devices  8.43 us (3%)
    pallas_call x1, Pallas kernels, per_device(): pl.pallas_call(functools.partial(grid_kernel, coils), grid=(blocks // til...  91.5 us
    pallas_call x1, Pallas kernels, per_device(): pl.pallas_call(functools.partial(add_kernel, chunk, span), grid_spec=pltp...  49.2 us
    all_to_all x1, waiting for transfers between devices, per_device(): split = lax.all_to_all(split, 'coil', 0, 0, tiled=True)  23.6 us
    all_to_all x1, blocking collectives, per_device(): split = lax.all_to_all(jnp.swapaxes(split, 0, 1), 'slab', 0, 0, tiled=True)  17.8 us
    pallas_call x1, Pallas kernels, per_device(): pl.pallas_call(sort_kernel, grid=(groups,), in_specs=[pl.BlockSpec((count...  16.5 us
    all_to_all x1, blocking collectives, per_device(): spots = lax.all_to_all(spots, 'slab', 0, 0, tiled=True).astype(jnp.int32)  11.9 us
    all_to_all x1, waiting for transfers between devices, per_device(): lax.all_to_all(ordered.reshape(slab_total, each, blocks), 'slab', 0, 0, t...  9.65 us
    reduce_sum x1, other arithmetic, per_device(): jnp.sum((key[:, :, None] < key[:, None, :]).astype(jnp.int32), axis=1)  8.06 us
  transfers between devices with their start and end apart: 2, of which 2 were waited for; matrix products, arithmetic and copies ran while one was open for 3% of the time, Pallas kernels for 0%

profile of v3, /device:TPU:0, one launch (start us, length us, event | category | flops | bytes accessed | tf_op | source)
XLA Modules:
  0.0 258.3 jit_solution(2222598133363714183)
XLA Ops:
  0.0 0.0 copy-start.1
  0.0 0.1 multiply_bitcast_fusion.1
  0.1 0.1 sine_multiply_fusion.1
  0.4 0.2 multiply_convert_fusion.2
  0.5 0.1 mul.391
  0.7 0.1 mul.402
  0.8 0.8 broadcast_multiply_fusion
  1.6 1.4 fusion.17
  3.1 8.1 %convert_reduce_fusion = s32[4,2048]{1,0:T(4,128)S(1)} fusion(s32[4,2048]{1,0:T(4,128)S(1)} %lt.95), kind=kLoop, calls=%fused_computation | loop fusion | flops 50323456 | bytes 65536 | tf_op jit(solution)/shard_map/reduce_sum | solution.py:207
  11.1 0.6 copy.34
  11.8 0.6 pad_maximum_fusion.5.tab_ref
  12.4 0.0 copy-done.1
  12.4 2.4 fusion.pos_ref
  14.8 0.8 fusion.8.spot_ref
  15.6 0.7 broadcast_in_dim.12.x_ref
  16.3 91.5 %grid_x.1.vals_ref = bf16[64,8192]{1,0:T(8,128)(2,1)} custom-call(f32[64,8192]{1,0:T(8,128)} %fusion.pos_ref, bf16[2,8192,128]{2,1,0:T(8,128)(2,1)} %val_ref.1, s32[1,8192]{1,0:T(1,128)} %bitcast.36, s32[64,128]{1,0:T(8,128)} %broadcast_in_dim.12.x_ref, bf16[128,256]{1,0:T(8,128)(2,1)} %pad_maximum_fusion.5.tab_ref), custom_call_target="tpu_custom_call" | custom-call | tf_op jit(solution)/shard_map/grid_x/pallas_call | solution.py:185
  107.8 16.5 %order_kz.1 = (bf16[64,8192]{1,0:T(8,128)(2,1)}, bf16[16,8192]{1,0:T(8,128)(2,1)}) custom-call(bf16[64,8192]{1,0:T(8,128)(2,1)} %grid_x.1.vals_ref, bf16[16,8192]{1,0:T(8,128)(2,1)} %fusion.8.spot_ref, s32[1,8192]{1,0:T(1,128)} %bitcast.38), custom_call_target="tpu_custom_call" | custom-call | tf_op jit(solution)/shard_map/order_kz/pallas_call | solution.py:210
  124.3 0.9 slice.22
  125.2 0.1 broadcast_in_dim.13
  125.4 11.9 %all_to_all.20 = bf16[8,2,8192]{2,1,0:T(2,128)(2,1)S(1)} all-to-all(bf16[8,2,8192]{2,1,0:T(2,128)(2,1)S(1)} %broadcast_in_dim.13), channel_id=1, replica_groups=mesh['slab'=8,'coil'=4] {'slab'}, dimensions={0} | all-to-all | bytes 524288 | tf_op jit(solution)/shard_map/all_to_all | solution.py:233
  137.3 3.6 %all-to-all-start.1 = ((bf16[8,8,8192]{2,1,0:T(8,128)(2,1)}), bf16[8,8,8192]{2,1,0:T(8,128)(2,1)S(1)}, u32[]{:S(2)}, u32[]{:S(2)}) async-start(bf16[8,8,8192]{2,1,0:T(8,128)(2,1)} %bitcast.35), calls=%async_computation.1 | async-start | bytes 2097152 | tf_op jit(solution)/shard_map/all_to_all | solution.py:229
  140.8 1.0 fusion.12
  141.8 1.1 negate_convert_fusion
  143.0 1.1 fusion.2
  144.0 0.2 convert_element_type.114
  144.2 1.4 fusion.45
  145.7 0.1 fusion.43
  145.9 0.6 fusion.36
  146.5 9.7 %all-to-all-done.1.vals_ref = bf16[8,8,8192]{2,1,0:T(8,128)(2,1)S(1)} async-done(((bf16[8,8,8192]{2,1,0:T(8,128)(2,1)}), bf16[8,8,8192]{2,1,0:T(8,128)(2,1)S(1)}, u32[]{:S(2)}, u32[]{:S(2)}) %all-to-all-start.1) | async-done | bytes 1048608 | tf_op jit(solution)/shard_map/all_to_all | solution.py:229
  156.2 0.0 copy-start
  156.2 1.0 copy-done
  157.1 49.2 %add_yz.1 = bf16[4,256,512]{2,1,0:T(8,128)(2,1)} custom-call(s32[256]{0:T(256)} %get-tuple-element.14.lo_ref, s32[256]{0:T(256)} %get-tuple-element.13.more_ref, bf16[8,8,8192]{2,1,0:T(8,128)(2,1)} %copy-done, s32[8,1,8192]{2,1,0:T(1,128)} %get-tuple-element.17.kz_ref, s32[8,1,8192]{2,1,0:T(1,128)} %get-tuple-element.15.ky_ref, ...), custom_call_target="tpu_custom_call" | custom-call | tf_op jit(solution)/shard_map/add_yz/pallas_call | solution.py:246
  206.4 1.3 copy.37
  207.7 17.8 %all_to_all.21 = bf16[8,4,32,512]{3,2,1,0:T(8,128)(2,1)S(1)} all-to-all(bf16[8,4,32,512]{3,2,1,0:T(8,128)(2,1)S(1)} %bitcast.33), channel_id=1, replica_groups=mesh['slab'=8,'coil'=4] {'slab'}, dimensions={0} | all-to-all | bytes 2097152 | tf_op jit(solution)/shard_map/all_to_all | solution.py:266
  225.5 1.1 copy.31
  226.5 4.9 %all-to-all-start.3 = ((bf16[4,4,2,32,512]{4,3,2,1,0:T(8,128)(2,1)}), bf16[4,4,2,32,512]{4,3,2,1,0:T(8,128)(2,1)S(1)}, u32[]{:S(2)}, u32[]{:S(2)}) async-start(bf16[4,4,2,32,512]{4,3,2,1,0:T(8,128)(2,1)} %bitcast.13), calls=%async_computation.3 | async-start | bytes 2097152 | tf_op jit(solution)/shard_map/all_to_all | solution.py:271
  231.4 1.5 copy_convert_fusion
  232.9 23.6 %all-to-all-done.3 = bf16[4,4,2,32,512]{4,3,2,1,0:T(8,128)(2,1)S(1)} async-done(((bf16[4,4,2,32,512]{4,3,2,1,0:T(8,128)(2,1)}), bf16[4,4,2,32,512]{4,3,2,1,0:T(8,128)(2,1)S(1)}, u32[]{:S(2)}, u32[]{:S(2)}) %all-to-all-start.3) | async-done | bytes 1048608 | tf_op jit(solution)/shard_map/all_to_all | solution.py:271
  256.6 0.3 convert_bitcast_fusion
  256.8 0.3 copy.32
  257.1 0.3 add_reduce_fusion
  257.5 0.9 copy.33
  (12 shorter events, 0.2 us)
Async XLA Ops:
  0.0 12.4 %copy-start.1 = (bf16[8192,64]{0,1:T(8,128)(2,1)S(1)}, bf16[8192,64]{0,1:T(8,128)(2,1)}, u32[]{:S(2)}) copy-start(bf16[8192,64]{0,1:T(8,128)(2,1)} %param.7) | copy-start | bytes 3145732
  137.3 18.9 %all-to-all-start.1 = ((bf16[8,8,8192]{2,1,0:T(8,128)(2,1)}), bf16[8,8,8192]{2,1,0:T(8,128)(2,1)S(1)}, u32[]{:S(2)}, u32[]{:S(2)}) async-start(bf16[8,8,8192]{2,1,0:T(8,128)(2,1)} %bitcast.35), calls=%async_computation.1 | async-start | bytes 2097152 | tf_op jit(solution)/shard_map/all_to_all | solution.py:229
  156.2 1.0 copy-start
  226.5 30.0 %all-to-all-start.3 = ((bf16[4,4,2,32,512]{4,3,2,1,0:T(8,128)(2,1)}), bf16[4,4,2,32,512]{4,3,2,1,0:T(8,128)(2,1)S(1)}, u32[]{:S(2)}, u32[]{:S(2)}) async-start(bf16[4,4,2,32,512]{4,3,2,1,0:T(8,128)(2,1)} %bitcast.13), calls=%async_computation.3 | async-start | bytes 2097152 | tf_op jit(solution)/shard_map/all_to_all | solution.py:271

commit v4 on v3

--- a/solution.py
+++ b/solution.py
@@ -81,8 +81,34 @@
         out_ref[:, cut] = jnp.where(turn >= 2, -turned, turned).astype(jnp.bfloat16)
 
 
-def sort_kernel(vals_ref, spot_ref, rank_ref, out_ref, spot_out_ref):
+def sort_kernel(vals_ref, spot_ref, kz_ref, out_ref, spot_out_ref, before, rank):
     rows, group = vals_ref.shape
+    depth = before.shape[0]
+    piece = math.gcd(128, group)
+    pieces = group // piece
+    level = lax.broadcasted_iota(jnp.int32, (depth, piece), 0)
+    src = lax.broadcasted_iota(jnp.int32, (piece, 2 * piece), 0)
+    dst = lax.broadcasted_iota(jnp.int32, (piece, 2 * piece), 1)
+    steps = jnp.where((src < dst) | (dst >= piece), 1.0, 0.0).astype(jnp.bfloat16)
+    seen = jnp.zeros((depth, piece), jnp.float32)
+    for at in range(pieces):
+        cut = slice(at * piece, (at + 1) * piece)
+        hot = jnp.where(level == kz_ref[:, cut], 1.0, 0.0)
+        counts = jnp.dot(hot.astype(jnp.bfloat16), steps, preferred_element_type=jnp.float32)
+        before[:, cut] = seen + counts[:, :piece]
+        seen = seen + counts[:, piece:]
+    high = jnp.floor(seen * (1.0 / 256.0))
+    low = seen - 256.0 * high
+    here = lax.broadcasted_iota(jnp.int32, (depth, depth), 0)
+    under = lax.broadcasted_iota(jnp.int32, (depth, depth), 1)
+    lower = jnp.where(under < here, 1.0, 0.0).astype(jnp.bfloat16)
+    first = 256.0 * jnp.dot(lower, high.astype(jnp.bfloat16), preferred_element_type=jnp.float32)
+    first = first + jnp.dot(lower, low.astype(jnp.bfloat16), preferred_element_type=jnp.float32)
+    for at in range(pieces):
+        cut = slice(at * piece, (at + 1) * piece)
+        found = jnp.where(level == kz_ref[:, cut], before[:, cut] + first, 0.0)
+        rank[:, cut] = jnp.sum(found, axis=0, keepdims=True).astype(jnp.int32)
+
     tile = math.gcd(256, group)
     slot = lax.broadcasted_iota(jnp.int32, (tile, group), 0)
     vals = jnp.concatenate([vals_ref[...], spot_ref[...]], axis=0)
@@ -90,7 +116,7 @@
     @pl.loop(0, group // tile)
     def _(at):
         start = pl.multiple_of(at * tile, tile)
-        hot = jnp.where(slot == (rank_ref[...] - start), 1.0, 0.0).astype(jnp.bfloat16)
+        hot = jnp.where(slot == (rank[...] - start), 1.0, 0.0).astype(jnp.bfloat16)
         moved = lax.dot_general(vals, hot, NT, preferred_element_type=jnp.float32)
         moved = moved.astype(jnp.bfloat16)
         out_ref[:, pl.ds(start, tile)] = moved[:rows]
@@ -203,9 +229,6 @@
 
     group = math.gcd(blocks, 2048)
     groups = blocks // group
-    key = (kz * group + ints(blocks) % group).reshape(groups, group)
-    rank = jnp.sum((key[:, :, None] < key[:, None, :]).astype(jnp.int32), axis=1)
-    rank = rank.reshape(1, blocks)
     spots = jnp.pad(jnp.stack([kz, ky]).astype(jnp.bfloat16), ((0, 14), (0, 0)))
     ordered, spots = pl.pallas_call(
         sort_kernel,
@@ -223,14 +246,22 @@
             jax.ShapeDtypeStruct((count, blocks), jnp.bfloat16),
             jax.ShapeDtypeStruct((16, blocks), jnp.bfloat16),
         ],
+        scratch_shapes=[
+            pltpu.VMEM((depth, group), jnp.float32),
+            pltpu.VMEM((1, group), jnp.int32),
+        ],
         name="order_kz",
-    )(lines, spots, rank)
+    )(lines, spots, kz[None, :])
     each = 2 * coils * x_here
+    tail = jnp.broadcast_to(spots[:2].reshape(1, each, -1), (slab_total, each, 2 * blocks // each))
     sent = lax.all_to_all(
-        ordered.reshape(slab_total, each, blocks), "slab", 0, 0, tiled=True
+        jnp.concatenate([ordered.reshape(slab_total, each, blocks), tail], axis=2),
+        "slab",
+        0,
+        0,
+        tiled=True,
     )
-    spots = jnp.broadcast_to(spots[:2][None], (slab_total, 2, blocks))
-    spots = lax.all_to_all(spots, "slab", 0, 0, tiled=True).astype(jnp.int32)
+    spots = sent[:, :, blocks:].reshape(slab_total, 2, blocks).astype(jnp.int32)
     kz_all = spots[:, 0:1]
     ky_all = spots[:, 1:2]
 

time: 262 us -> 253 us (0.966)
  blocking collectives: 29.7 us -> 17.8 us
  waiting for transfers between devices: 33.3 us -> 38.7 us
  other arithmetic: 20.8 us -> 15.4 us
  Pallas kernels: 157 us -> 160 us
    all_to_all x1 -> x0, blocking collectives: 11.9 us -> none  [per_device(): spots = lax.all_to_all(spots, 'slab', 0, 0, tiled=True).astype(jnp.int32)]
    reduce_sum x1 -> x0, other arithmetic: 8.06 us -> none  [per_device(): jnp.sum((key[:, :, None] < key[:, None, :]).astype(jnp.int32), axis=1)]
    all_to_all x1, waiting for transfers between devices: 9.65 us -> 15 us  [per_device(): lax.all_to_all(jnp.concatenate([ordered.reshape(slab_total, each, blocks)...]
    pallas_call x1, Pallas kernels: 16.5 us -> 21.2 us  [per_device(): pl.pallas_call(sort_kernel, grid=(groups,), in_specs=[pl.BlockSpec((count...]
  transfers between devices with their start and end apart: 2 -> 2, of which waited for: 2 -> 2; matrix products, arithmetic and copies ran while one was open for 3% -> 2% of each run, Pallas kernels for 0% -> 0%
where the time goes in v4:
time: 253 us; the launch traced here: 250 us
  Pallas kernels  160 us (63%)
  waiting for transfers between devices  38.7 us (15%)
  blocking collectives  17.8 us (7%)
  other arithmetic  15.4 us (6%)
  starting transfers between devices  10.1 us (4%)
  local copies, waits for them, and re-layouts  7.29 us (3%)
    pallas_call x1, Pallas kernels, per_device(): pl.pallas_call(functools.partial(grid_kernel, coils), grid=(blocks // til...  91.5 us
    pallas_call x1, Pallas kernels, per_device(): pl.pallas_call(functools.partial(add_kernel, chunk, span), grid_spec=pltp...  47.5 us
    all_to_all x1, waiting for transfers between devices, per_device(): split = lax.all_to_all(split, 'coil', 0, 0, tiled=True)  23.6 us
    pallas_call x1, Pallas kernels, per_device(): pl.pallas_call(sort_kernel, grid=(groups,), in_specs=[pl.BlockSpec((count...  21.2 us
    all_to_all x1, blocking collectives, per_device(): split = lax.all_to_all(jnp.swapaxes(split, 0, 1), 'slab', 0, 0, tiled=True)  17.8 us
    all_to_all x1, waiting for transfers between devices, per_device(): lax.all_to_all(jnp.concatenate([ordered.reshape(slab_total, each, blocks)...  15 us
    all_to_all x1, starting transfers between devices, per_device(): lax.all_to_all(jnp.concatenate([ordered.reshape(slab_total, each, blocks)...  5.2 us
  transfers between devices with their start and end apart: 2, of which 2 were waited for; matrix products, arithmetic and copies ran while one was open for 2% of the time, Pallas kernels for 0%

profile of v4, /device:TPU:0, one launch (start us, length us, event | category | flops | bytes accessed | tf_op | source)
XLA Modules:
  0.0 249.5 jit_solution(12282039842912447489)
XLA Ops:
  0.0 0.1 multiply_bitcast_fusion.1
  0.1 0.1 sine_multiply_fusion.1
  0.4 0.2 multiply_convert_fusion.2
  0.5 0.1 mul.385
  0.7 0.1 mul.396
  0.8 0.8 broadcast_multiply_fusion
  1.6 1.4 fusion.14
  3.0 0.0 copy-start.1
  3.0 0.6 pad_maximum_fusion.6.tab_ref
  3.7 2.8 %fusion.pos_ref = f32[64,8192]{1,0:T(8,128)} fusion(bf16[8192,64]{0,1:T(8,128)(2,1)} %param.7, s32[8192]{0:T(1024)} %param.8), kind=kLoop, calls=%fused_computation.1 | loop fusion | flops 2097152 | bytes 3178496 | tf_op jit(solution)/shard_map/mul | solution.py:200
  6.5 0.8 fusion.8.spot_ref
  7.3 0.7 broadcast_in_dim.14.x_ref
  8.0 91.5 %grid_x.1.vals_ref = bf16[64,8192]{1,0:T(8,128)(2,1)} custom-call(f32[64,8192]{1,0:T(8,128)} %fusion.pos_ref, bf16[2,8192,128]{2,1,0:T(8,128)(2,1)} %val_ref.1, s32[1,8192]{1,0:T(1,128)} %bitcast.36, s32[64,128]{1,0:T(8,128)} %broadcast_in_dim.14.x_ref, bf16[128,256]{1,0:T(8,128)(2,1)} %pad_maximum_fusion.6.tab_ref), custom_call_target="tpu_custom_call" | custom-call | tf_op jit(solution)/shard_map/grid_x/pallas_call | solution.py:211
  99.5 0.0 copy-done.1
  99.5 21.2 %order_kz.1 = (bf16[64,8192]{1,0:T(8,128)(2,1)}, bf16[16,8192]{1,0:T(8,128)(2,1)}) custom-call(bf16[64,8192]{1,0:T(8,128)(2,1)} %grid_x.1.vals_ref, bf16[16,8192]{1,0:T(8,128)(2,1)} %fusion.8.spot_ref, s32[1,8192]{1,0:T(1,128)} %bitcast.35), custom_call_target="tpu_custom_call" | custom-call | tf_op jit(solution)/shard_map/order_kz/pallas_call | solution.py:233
  120.7 0.9 slice.25
  121.7 2.4 pad_maximum_fusion
  124.0 5.2 %all-to-all-start = ((bf16[8,8,10240]{2,1,0:T(8,128)(2,1)}), bf16[8,8,10240]{2,1,0:T(8,128)(2,1)S(1)}, u32[]{:S(2)}, u32[]{:S(2)}) async-start(bf16[8,8,10240]{2,1,0:T(8,128)(2,1)} %pad_maximum_fusion), calls=%async_computation | async-start | bytes 2621440 | tf_op jit(solution)/shard_map/all_to_all | solution.py:257
  129.2 1.0 fusion.12
  130.2 1.1 negate_convert_fusion
  131.4 1.0 fusion.2
  132.4 15.0 %all-to-all-done.vals_ref = bf16[8,8,10240]{2,1,0:T(8,128)(2,1)S(1)} async-done(((bf16[8,8,10240]{2,1,0:T(8,128)(2,1)}), bf16[8,8,10240]{2,1,0:T(8,128)(2,1)S(1)}, u32[]{:S(2)}, u32[]{:S(2)}) %all-to-all-start) | async-done | bytes 1310752 | tf_op jit(solution)/shard_map/all_to_all | solution.py:257
  147.4 0.0 copy-start
  147.4 0.1 slice_convert_fusion
  147.5 0.4 reshape.301
  147.9 1.4 fusion.40
  149.4 0.1 fusion.38
  149.5 0.6 fusion.32
  150.2 0.0 copy-done
  150.2 47.5 %add_yz.1 = bf16[4,256,512]{2,1,0:T(8,128)(2,1)} custom-call(s32[256]{0:T(256)} %get-tuple-element.14.lo_ref, s32[256]{0:T(256)} %get-tuple-element.13.more_ref, bf16[8,8,10240]{2,1,0:T(8,128)(2,1)} %copy-done, s32[8,1,8192]{2,1,0:T(1,128)} %get-tuple-element.17.kz_ref, s32[8,1,8192]{2,1,0:T(1,128)} %get-tuple-element.15.ky_ref, ...), custom_call_target="tpu_custom_call" | custom-call | tf_op jit(solution)/shard_map/add_yz/pallas_call | solution.py:277
  197.6 1.3 copy.30
  198.9 17.8 %all_to_all.15 = bf16[8,4,32,512]{3,2,1,0:T(8,128)(2,1)S(1)} all-to-all(bf16[8,4,32,512]{3,2,1,0:T(8,128)(2,1)S(1)} %bitcast.31), channel_id=1, replica_groups=mesh['slab'=8,'coil'=4] {'slab'}, dimensions={0} | all-to-all | bytes 2097152 | tf_op jit(solution)/shard_map/all_to_all | solution.py:297
  216.7 1.0 copy.25
  217.7 4.9 %all-to-all-start.2 = ((bf16[4,4,2,32,512]{4,3,2,1,0:T(8,128)(2,1)}), bf16[4,4,2,32,512]{4,3,2,1,0:T(8,128)(2,1)S(1)}, u32[]{:S(2)}, u32[]{:S(2)}) async-start(bf16[4,4,2,32,512]{4,3,2,1,0:T(8,128)(2,1)} %bitcast.14), calls=%async_computation.2 | async-start | bytes 2097152 | tf_op jit(solution)/shard_map/all_to_all | solution.py:302
  222.6 1.5 copy_convert_fusion
  224.1 23.6 %all-to-all-done.2 = bf16[4,4,2,32,512]{4,3,2,1,0:T(8,128)(2,1)S(1)} async-done(((bf16[4,4,2,32,512]{4,3,2,1,0:T(8,128)(2,1)}), bf16[4,4,2,32,512]{4,3,2,1,0:T(8,128)(2,1)S(1)}, u32[]{:S(2)}, u32[]{:S(2)}) %all-to-all-start.2) | async-done | bytes 1048608 | tf_op jit(solution)/shard_map/all_to_all | solution.py:302
  247.7 0.3 convert_bitcast_fusion
  248.0 0.3 copy.26
  248.3 0.3 add_reduce_fusion
  248.6 0.9 copy.27
  (13 shorter events, 0.2 us)
Async XLA Ops:
  3.0 96.5 %copy-start.1 = (s32[8192]{0:T(1024)}, s32[8192]{0:T(1024)S(1)}, u32[]{:S(2)}) copy-start(s32[8192]{0:T(1024)S(1)} %get-tuple-element.20) | copy-start | bytes 98308
  124.0 23.4 %all-to-all-start = ((bf16[8,8,10240]{2,1,0:T(8,128)(2,1)}), bf16[8,8,10240]{2,1,0:T(8,128)(2,1)S(1)}, u32[]{:S(2)}, u32[]{:S(2)}) async-start(bf16[8,8,10240]{2,1,0:T(8,128)(2,1)} %pad_maximum_fusion), calls=%async_computation | async-start | bytes 2621440 | tf_op jit(solution)/shard_map/all_to_all | solution.py:257
  147.4 2.7 %copy-start = (bf16[8,8,10240]{2,1,0:T(8,128)(2,1)}, bf16[8,8,10240]{2,1,0:T(8,128)(2,1)S(1)}, u32[]{:S(2)}) copy-start(bf16[8,8,10240]{2,1,0:T(8,128)(2,1)S(1)} %all-to-all-done.vals_ref) | copy-start | bytes 3932164
  217.7 30.0 %all-to-all-start.2 = ((bf16[4,4,2,32,512]{4,3,2,1,0:T(8,128)(2,1)}), bf16[4,4,2,32,512]{4,3,2,1,0:T(8,128)(2,1)S(1)}, u32[]{:S(2)}, u32[]{:S(2)}) async-start(bf16[4,4,2,32,512]{4,3,2,1,0:T(8,128)(2,1)} %bitcast.14), calls=%async_computation.2 | async-start | bytes 2097152 | tf_op jit(solution)/shard_map/all_to_all | solution.py:302

commit v5 on v4

--- a/solution.py
+++ b/solution.py
@@ -73,7 +73,7 @@
             )
 
         zero = jnp.zeros((CELLS, lanes), jnp.float32)
-        sums = lax.fori_loop(0, CELLS, step, (zero,) * (2 * coils), unroll=4)
+        sums = lax.fori_loop(0, CELLS, step, (zero,) * (2 * coils), unroll=16)
         turn = (x_ref[...] * seg_ref[:, cut]) & 3
         cells = jnp.concatenate([part.astype(jnp.bfloat16) for part in sums], axis=0)
         moved = jnp.dot(tab_ref[...], cells, preferred_element_type=jnp.float32)

time: 253 us -> 249 us (0.984)
  Pallas kernels: 160 us -> 156 us
    pallas_call x1, Pallas kernels: 91.5 us -> 86.2 us  [per_device(): pl.pallas_call(functools.partial(grid_kernel, coils), grid=(blocks // til...]
where the time goes in v5:
time: 249 us; the launch traced here: 245 us
  Pallas kernels  156 us (63%)
  waiting for transfers between devices  38.7 us (16%)
  blocking collectives  17.8 us (7%)
  other arithmetic  15.4 us (6%)
  starting transfers between devices  10.1 us (4%)
  local copies, waits for them, and re-layouts  7.29 us (3%)
    pallas_call x1, Pallas kernels, per_device(): pl.pallas_call(functools.partial(grid_kernel, coils), grid=(blocks // til...  86.2 us
    pallas_call x1, Pallas kernels, per_device(): pl.pallas_call(functools.partial(add_kernel, chunk, span), grid_spec=pltp...  48.5 us
    all_to_all x1, waiting for transfers between devices, per_device(): split = lax.all_to_all(split, 'coil', 0, 0, tiled=True)  23.6 us
    pallas_call x1, Pallas kernels, per_device(): pl.pallas_call(sort_kernel, grid=(groups,), in_specs=[pl.BlockSpec((count...  21.2 us
    all_to_all x1, blocking collectives, per_device(): split = lax.all_to_all(jnp.swapaxes(split, 0, 1), 'slab', 0, 0, tiled=True)  17.8 us
    all_to_all x1, waiting for transfers between devices, per_device(): lax.all_to_all(jnp.concatenate([ordered.reshape(slab_total, each, blocks)...  15 us
    all_to_all x1, starting transfers between devices, per_device(): lax.all_to_all(jnp.concatenate([ordered.reshape(slab_total, each, blocks)...  5.2 us
  transfers between devices with their start and end apart: 2, of which 2 were waited for; matrix products, arithmetic and copies ran while one was open for 2% of the time, Pallas kernels for 0%

profile of v5, /device:TPU:0, one launch (start us, length us, event | category | flops | bytes accessed | tf_op | source)
XLA Modules:
  0.0 245.3 jit_solution(11712285020338861472)
XLA Ops:
  0.0 0.1 multiply_bitcast_fusion.1
  0.1 0.1 sine_multiply_fusion.1
  0.4 0.2 multiply_convert_fusion.2
  0.5 0.1 mul.385
  0.7 0.1 mul.396
  0.8 0.8 broadcast_multiply_fusion
  1.6 1.4 fusion.14
  3.0 0.0 copy-start.1
  3.0 0.6 pad_maximum_fusion.6.tab_ref
  3.7 2.8 %fusion.pos_ref = f32[64,8192]{1,0:T(8,128)} fusion(bf16[8192,64]{0,1:T(8,128)(2,1)} %param.7, s32[8192]{0:T(1024)} %param.8), kind=kLoop, calls=%fused_computation.1 | loop fusion | flops 2097152 | bytes 3178496 | tf_op jit(solution)/shard_map/mul | solution.py:200
  6.5 0.8 fusion.8.spot_ref
  7.3 0.7 broadcast_in_dim.14.x_ref
  8.0 86.2 %grid_x.1.vals_ref = bf16[64,8192]{1,0:T(8,128)(2,1)} custom-call(f32[64,8192]{1,0:T(8,128)} %fusion.pos_ref, bf16[2,8192,128]{2,1,0:T(8,128)(2,1)} %val_ref.1, s32[1,8192]{1,0:T(1,128)} %bitcast.36, s32[64,128]{1,0:T(8,128)} %broadcast_in_dim.14.x_ref, bf16[128,256]{1,0:T(8,128)(2,1)} %pad_maximum_fusion.6.tab_ref), custom_call_target="tpu_custom_call" | custom-call | tf_op jit(solution)/shard_map/grid_x/pallas_call | solution.py:211
  94.2 0.0 copy-done.1
  94.2 21.2 %order_kz.1 = (bf16[64,8192]{1,0:T(8,128)(2,1)}, bf16[16,8192]{1,0:T(8,128)(2,1)}) custom-call(bf16[64,8192]{1,0:T(8,128)(2,1)} %grid_x.1.vals_ref, bf16[16,8192]{1,0:T(8,128)(2,1)} %fusion.8.spot_ref, s32[1,8192]{1,0:T(1,128)} %bitcast.35), custom_call_target="tpu_custom_call" | custom-call | tf_op jit(solution)/shard_map/order_kz/pallas_call | solution.py:233
  115.4 0.9 slice.25
  116.4 2.4 pad_maximum_fusion
  118.8 5.2 %all-to-all-start = ((bf16[8,8,10240]{2,1,0:T(8,128)(2,1)}), bf16[8,8,10240]{2,1,0:T(8,128)(2,1)S(1)}, u32[]{:S(2)}, u32[]{:S(2)}) async-start(bf16[8,8,10240]{2,1,0:T(8,128)(2,1)} %pad_maximum_fusion), calls=%async_computation | async-start | bytes 2621440 | tf_op jit(solution)/shard_map/all_to_all | solution.py:257
  124.0 1.0 fusion.12
  125.0 1.1 negate_convert_fusion
  126.1 1.0 fusion.2
  127.1 15.0 %all-to-all-done.vals_ref = bf16[8,8,10240]{2,1,0:T(8,128)(2,1)S(1)} async-done(((bf16[8,8,10240]{2,1,0:T(8,128)(2,1)}), bf16[8,8,10240]{2,1,0:T(8,128)(2,1)S(1)}, u32[]{:S(2)}, u32[]{:S(2)}) %all-to-all-start) | async-done | bytes 1310752 | tf_op jit(solution)/shard_map/all_to_all | solution.py:257
  142.2 0.0 copy-start
  142.2 0.1 slice_convert_fusion
  142.2 0.4 reshape.301
  142.6 1.4 fusion.40
  144.1 0.1 fusion.38
  144.3 0.6 fusion.32
  144.9 0.0 copy-done
  144.9 48.5 %add_yz.1 = bf16[4,256,512]{2,1,0:T(8,128)(2,1)} custom-call(s32[256]{0:T(256)} %get-tuple-element.14.lo_ref, s32[256]{0:T(256)} %get-tuple-element.13.more_ref, bf16[8,8,10240]{2,1,0:T(8,128)(2,1)} %copy-done, s32[8,1,8192]{2,1,0:T(1,128)} %get-tuple-element.17.kz_ref, s32[8,1,8192]{2,1,0:T(1,128)} %get-tuple-element.15.ky_ref, ...), custom_call_target="tpu_custom_call" | custom-call | tf_op jit(solution)/shard_map/add_yz/pallas_call | solution.py:277
  193.4 1.3 copy.30
  194.7 17.8 %all_to_all.15 = bf16[8,4,32,512]{3,2,1,0:T(8,128)(2,1)S(1)} all-to-all(bf16[8,4,32,512]{3,2,1,0:T(8,128)(2,1)S(1)} %bitcast.31), channel_id=1, replica_groups=mesh['slab'=8,'coil'=4] {'slab'}, dimensions={0} | all-to-all | bytes 2097152 | tf_op jit(solution)/shard_map/all_to_all | solution.py:297
  212.5 1.0 copy.25
  213.5 4.9 %all-to-all-start.2 = ((bf16[4,4,2,32,512]{4,3,2,1,0:T(8,128)(2,1)}), bf16[4,4,2,32,512]{4,3,2,1,0:T(8,128)(2,1)S(1)}, u32[]{:S(2)}, u32[]{:S(2)}) async-start(bf16[4,4,2,32,512]{4,3,2,1,0:T(8,128)(2,1)} %bitcast.14), calls=%async_computation.2 | async-start | bytes 2097152 | tf_op jit(solution)/shard_map/all_to_all | solution.py:302
  218.4 1.5 copy_convert_fusion
  219.9 23.6 %all-to-all-done.2 = bf16[4,4,2,32,512]{4,3,2,1,0:T(8,128)(2,1)S(1)} async-done(((bf16[4,4,2,32,512]{4,3,2,1,0:T(8,128)(2,1)}), bf16[4,4,2,32,512]{4,3,2,1,0:T(8,128)(2,1)S(1)}, u32[]{:S(2)}, u32[]{:S(2)}) %all-to-all-start.2) | async-done | bytes 1048608 | tf_op jit(solution)/shard_map/all_to_all | solution.py:302
  243.5 0.3 convert_bitcast_fusion
  243.8 0.3 copy.26
  244.1 0.3 add_reduce_fusion
  244.4 0.9 copy.27
  (13 shorter events, 0.2 us)
Async XLA Ops:
  3.0 91.2 %copy-start.1 = (s32[8192]{0:T(1024)}, s32[8192]{0:T(1024)S(1)}, u32[]{:S(2)}) copy-start(s32[8192]{0:T(1024)S(1)} %get-tuple-element.20) | copy-start | bytes 98308
  118.8 23.4 %all-to-all-start = ((bf16[8,8,10240]{2,1,0:T(8,128)(2,1)}), bf16[8,8,10240]{2,1,0:T(8,128)(2,1)S(1)}, u32[]{:S(2)}, u32[]{:S(2)}) async-start(bf16[8,8,10240]{2,1,0:T(8,128)(2,1)} %pad_maximum_fusion), calls=%async_computation | async-start | bytes 2621440 | tf_op jit(solution)/shard_map/all_to_all | solution.py:257
  142.2 2.7 %copy-start = (bf16[8,8,10240]{2,1,0:T(8,128)(2,1)}, bf16[8,8,10240]{2,1,0:T(8,128)(2,1)S(1)}, u32[]{:S(2)}) copy-start(bf16[8,8,10240]{2,1,0:T(8,128)(2,1)S(1)} %all-to-all-done.vals_ref) | copy-start | bytes 3932164
  213.5 30.0 %all-to-all-start.2 = ((bf16[4,4,2,32,512]{4,3,2,1,0:T(8,128)(2,1)}), bf16[4,4,2,32,512]{4,3,2,1,0:T(8,128)(2,1)S(1)}, u32[]{:S(2)}, u32[]{:S(2)}) async-start(bf16[4,4,2,32,512]{4,3,2,1,0:T(8,128)(2,1)} %bitcast.14), calls=%async_computation.2 | async-start | bytes 2097152 | tf_op jit(solution)/shard_map/all_to_all | solution.py:302
